TPU v7x, 32 devices: a whole 2x2x4 slice. The times are simulated.
32 devices in a mesh: row: 4 (over x, core), col: 8 (over z, y).
Axes of the slice: x: 2, y: 2, z: 4, core: 2. Of those that a mesh axis runs over, the one named last changes fastest.
Arguments:
- gradients: bfloat16 [8, 4, 8, 32, 512], P(None, 'row', 'col'), may hold values from -2.5 to 2.5
- feature_weights: float32 [512], replicated, may hold values from 0.005859375 to 0.029296875
- order: int32 [8, 4, 256], P(None, 'row'), may hold values from 0 to 255, each once within a row
Outputs:
- factored: float32 [8, 4, 4, 8, 256, 256], P(None, 'row', None, 'col')
Inputs may be any that keep to these rules, and one draw needn't show every extreme that they name: Each order[a, r, :] is a permutation of 0 to 255.
All inputs are finite; a program needn't handle non-finite values.
Results may differ from a plain program's by a relative error of at most 0.0025.
Values may be sent and summed in bfloat16 or wider, within the bound.
A program may use at most 64 MiB of HBM per device.

v0:
```python
import jax
import jax.numpy as jnp
from jax import lax
from jax.sharding import PartitionSpec as P

RIDGE = 0.5
EXACT = lax.Precision.HIGHEST


def broadcast(value, axis, source):
    kept = jnp.where(lax.axis_index(axis) == source, value, 0).astype(value.dtype)
    return lax.psum(kept, axis)


def scale_rows(blocks, feature_weights):
    widened = blocks.astype(jnp.float32)
    scaled = lax.optimization_barrier((widened * feature_weights).astype(jnp.bfloat16))
    squares = jnp.sum(scaled.astype(jnp.float32) * widened, axis=-1)
    return (scaled, squares)


def kernel_blocks(left_side, left_squares, right_side, right_squares):
    products = jnp.einsum(
        "aip,bjp->abij", left_side, right_side, preferred_element_type=jnp.float32
    )
    distance = left_squares[:, None, :, None] + right_squares[None, :, None, :] - 2.0 * products
    return jnp.exp(-0.5 * distance)


def add_ridge(tile_set, row_labels, col_labels):
    diagonal = (row_labels[:, None] == col_labels[None, :]).astype(jnp.float32)
    identity = jnp.eye(tile_set.shape[-1], dtype=jnp.float32)
    return tile_set + RIDGE * diagonal[:, :, None, None] * identity


def right_solve(factor, tile_set):
    number = tile_set.shape[0]
    size_b = tile_set.shape[-1]
    stacked = tile_set.reshape(number * size_b, size_b)
    solved = lax.linalg.triangular_solve(
        factor, stacked, left_side=False, lower=True, transpose_a=True
    )
    return solved.reshape(number, size_b, size_b)


def outer_update(current, row_factors, col_factors):
    return current - jnp.einsum("aik,bjk->abij", row_factors, col_factors, precision=EXACT)


def pick_cols(blocks, col_index, row_count, col_ratio):
    grouped = blocks.reshape((blocks.shape[0] // col_ratio, col_ratio) + blocks.shape[1:])
    return lax.dynamic_index_in_dim(grouped, col_index // row_count, axis=1, keepdims=False)


def lead_factors(leaders, lead_scaled, lead_squares):
    lead_ids = jnp.arange(2, dtype=jnp.int32)
    corner = add_ridge(
        kernel_blocks(lead_scaled, lead_squares, leaders, lead_squares), lead_ids, lead_ids
    )
    lower_first = jnp.linalg.cholesky(corner[0, 0])
    below_factor = right_solve(lower_first, corner[1:, 0])[0]
    reduced = corner[1, 1] - jnp.dot(below_factor, below_factor.T, precision=EXACT)
    return (lower_first, below_factor, jnp.linalg.cholesky(reduced))


def panel_pair(
    scaled, squares, labels, leaders, lead_squares, lower_first, below_factor, lower_second
):
    lead_ids = jnp.arange(2, dtype=jnp.int32)
    tile_set = add_ridge(kernel_blocks(scaled, squares, leaders, lead_squares), labels, lead_ids)
    first_panel = right_solve(lower_first, tile_set[:, 0])
    second_panel = tile_set[:, 1] - jnp.einsum(
        "aik,jk->aij", first_panel, below_factor, precision=EXACT
    )
    second_panel = right_solve(lower_second, second_panel)
    first_panel = jnp.where((labels == 0)[:, None, None], lower_first, first_panel)
    second_panel = jnp.where((labels == 1)[:, None, None], lower_second, second_panel)
    second_panel = jnp.where((labels == 0)[:, None, None], 0.0, second_panel)
    return (first_panel, second_panel)


def per_device(gradients, feature_weights, order):
    row_count = lax.axis_size("row")
    col_count = lax.axis_size("col")
    row_index = lax.axis_index("row")
    col_index = lax.axis_index("col")
    col_ratio = col_count // row_count
    gathered = lax.all_gather(gradients, "col", axis=2, tiled=True)
    local_rows = gathered.shape[0]
    size_b = gathered.shape[2] * gathered.shape[3]
    feature_count = gathered.shape[4]
    stacked = gathered.reshape(local_rows, size_b, feature_count)
    slot_ids = order.reshape(local_rows, size_b)
    own_rows = jnp.take_along_axis(stacked, slot_ids[:, :, None], axis=1)
    own_cols = broadcast(
        pick_cols(own_rows, col_index, row_count, col_ratio), "row", col_index % row_count
    )
    local_cols = own_cols.shape[0]
    row_labels = jnp.arange(local_rows, dtype=jnp.int32) * row_count + row_index
    col_labels = jnp.arange(local_cols, dtype=jnp.int32) * col_count + col_index
    scaled_rows, squares_rows = scale_rows(own_rows, feature_weights)
    scaled_cols, squares_cols = scale_rows(own_cols, feature_weights)
    matrix = add_ridge(
        kernel_blocks(scaled_rows, squares_rows, own_cols, squares_cols), row_labels, col_labels
    )
    leaders = lax.all_gather(own_rows[:1], "row", axis=0, tiled=True)[:2]
    lead_scaled, lead_squares = scale_rows(leaders, feature_weights)
    lower_first, below_factor, lower_second = lead_factors(leaders, lead_scaled, lead_squares)
    rows_first, rows_second = panel_pair(
        scaled_rows,
        squares_rows,
        row_labels,
        leaders,
        lead_squares,
        lower_first,
        below_factor,
        lower_second,
    )
    cols_first, cols_second = panel_pair(
        scaled_cols,
        squares_cols,
        col_labels,
        leaders,
        lead_squares,
        lower_first,
        below_factor,
        lower_second,
    )
    trailing = outer_update(outer_update(matrix, rows_first, cols_first), rows_second, cols_second)
    upper_rows = row_labels < 2
    trailing = jnp.where(upper_rows[:, None, None, None], 0.0, trailing)
    leading = jnp.where(col_index == 0, rows_first, rows_second)
    result = jnp.where((col_labels < 2)[None, :, None, None], leading[:, None], trailing)
    return result.reshape(local_rows, 1, local_cols, 1, size_b, size_b)


def solution(mesh):
    placed = (P(None, "row", "col", None, None), P(), P(None, "row", None))
    return jax.shard_map(
        per_device,
        mesh=mesh,
        in_specs=placed,
        out_specs=P(None, "row", None, "col", None, None),
        check_vma=False,
    )
```

profile of v0, /device:TPU:0, one launch (start us, length us, event | category | flops | bytes accessed | tf_op | source)
XLA Modules:
  0.0 393.8 jit_solution(8190877837483084400)
XLA Ops:
  10.8 50.7 %all-gather.3.cloned.1.call-done = bf16[8,1,8,32,512]{4,3,2,1,0:T(8,128)(2,1)} async-done(((bf16[8,1,1,32,512]{4,3,2,1,0:T(8,128)(2,1)}), bf16[8,1,8,32,512]{4,3,2,1,0:T(8,128)(2,1)}) %all-gather.3.cloned.1.call-update) | async-done | bytes 2097168 | tf_op jit(solution)/shard_map/all_gather | solution.py:88
  61.5 26.4 %gather_fusion = bf16[2048,512]{1,0:T(8,128)(2,1)S(1)} fusion(bf16[8,256,512]{2,1,0:T(8,128)(2,1)} %bitcast.270, s32[2048]{0:T(1024)S(1)} %bitcast.269), kind=kCustom, calls=%fused_computation | custom fusion | bytes 4210688 | tf_op jit(solution)/shard_map/jit(take_along_axis)/gather | solution.py:94
  88.0 1.4 fusion.34
  91.9 2.1 fusion.6
  94.0 1.3 copy-done
  98.4 2.9 fusion.7
  101.3 23.0 %all-reduce.3.cloned.1.call-done = bf16[4,256,512]{2,1,0:T(8,128)(2,1)} async-done(((bf16[4,256,512]{2,1,0:T(8,128)(2,1)}), bf16[4,256,512]{2,1,0:T(8,128)(2,1)}) %all-reduce.3.cloned.1.call-update) | async-done | bytes 1048592 | tf_op jit(solution)/shard_map/psum | solution.py:12
  124.3 1.5 fusion.11
  125.8 1.1 copy-done.15
  127.9 15.2 %all-gather.5.cloned.1.call-done = bf16[4,256,512]{2,1,0:T(8,128)(2,1)} async-done(((bf16[1,256,512]{2,1,0:T(8,128)(2,1)}), bf16[4,256,512]{2,1,0:T(8,128)(2,1)}) %all-gather.5.cloned.1.call-update) | async-done | bytes 1048592 | tf_op jit(solution)/shard_map/all_gather | solution.py:106
  143.1 1.2 fusion.31
  144.3 1.3 fusion.32
  147.1 1.2 copy.52
  149.1 11.7 %cholesky.130 = f32[128,128]{1,0:T(8,128)S(1)} custom-call(f32[128,128]{1,0:T(8,128)S(1)} %cholesky.194), custom_call_target="Cholesky" | custom-call | tf_op jit(solution)/shard_map/jit(cholesky)/cholesky | solution.py:60
  161.4 9.8 %custom-call.23 = f32[1,128,128]{1,2,0:T(8,128)S(1)} custom-call(f32[1,128,128]{2,1,0:T(8,128)S(1)} %get-tuple-element.89), custom_call_target="InvertDiagBlocksLowerTriangular" | custom-call | tf_op jit(solution)/shard_map/jit(cholesky)/cholesky | solution.py:60
  171.2 1.0 constant_dynamic-update-slice_fusion.2
  172.3 1.1 convolution_subtract_fusion.8
  173.4 22.2 %cholesky.147 = f32[128,128]{1,0:T(8,128)S(1)} custom-call(f32[128,128]{1,0:T(8,128)S(1)} %convolution_subtract_fusion.8), custom_call_target="Cholesky" | custom-call | tf_op jit(solution)/shard_map/jit(cholesky)/cholesky | solution.py:60
  195.7 1.3 compare_reduce_fusion.2
  198.3 1.7 fusion.58
  200.8 4.1 %while.9 = (s32[]{:T(128)}, f32[256,256]{1,0:T(8,128)S(1)}, s32[2,2]{1,0:T(2,128)S(1)}, f32[2,128,128]{2,1,0:T(8,128)S(1)}, s32[]{:T(128)}) while((s32[]{:T(128)}, f32[256,256]{1,0:T(8,128)S(1)}, s32[2,2]{1,0:T(2,128)S(1)}, f32[2,128,128]{2,1,0:T(8,128)S(1)}, s32[]{:T(128)}) %tuple.63), condition=%wide.while_cond, body=%wide.while_body.sunk | while | flops 2 | bytes 131181 | solution.py:40
  201.4 1.4 bitcast_dynamic-update-slice_fusion.4
  203.5 1.4 bitcast_dynamic-update-slice_fusion.4
  205.5 19.7 %custom-call.24 = f32[2,128,128]{1,2,0:T(8,128)S(1)} custom-call(f32[2,128,128]{2,1,0:T(8,128)S(1)} %get-tuple-element.44), custom_call_target="InvertDiagBlocksLowerTriangular" | custom-call | tf_op jit(solution)/shard_map/triangular_solve/custom-call.0 | solution.py:40
  225.2 3.1 fusion.10
  228.5 1.9 copy-done.11
  230.3 1.1 fusion.37
  231.4 1.8 convolution_subtract_fusion.1
  233.3 2.1 fusion.74
  237.0 1.1 convolution_subtract_fusion.6
  238.4 2.3 convolution_subtract_fusion.5
  240.7 1.7 broadcast_select_fusion.1
  242.5 1.2 copy-done.12
  243.7 5.2 %fusion.18 = f32[8,256,256]{2,1,0:T(8,128)} fusion(f32[8,2,256,256]{3,2,0,1:T(8,128)S(1)} %copy-done.12, f32[32,8,8,256]{3,2,1,0:T(8,128)S(1)} %bitcast.271, f32[256,128]{0,1:T(8,128)S(1)} %fusion.73, f32[256,128]{0,1:T(8,128)S(1)} %fusion.60), kind=kOutput, calls=%fused_computation.36 | convolution fusion | flops 1611202560 | bytes 6553600 | tf_op jit(solution)/shard_map/aik,jk->aij/dot_general | solution.py:72
  249.0 11.7 %cholesky.164 = f32[128,128]{1,0:T(8,128)S(1)} custom-call(f32[128,128]{1,0:T(8,128)S(1)} %cholesky.197), custom_call_target="Cholesky" | custom-call | tf_op jit(solution)/shard_map/jit(cholesky)/cholesky | solution.py:63
  260.8 9.8 %custom-call.25 = f32[1,128,128]{1,2,0:T(8,128)S(1)} custom-call(f32[1,128,128]{2,1,0:T(8,128)S(1)} %get-tuple-element.85), custom_call_target="InvertDiagBlocksLowerTriangular" | custom-call | tf_op jit(solution)/shard_map/jit(cholesky)/cholesky | solution.py:63
  271.1 11.7 %cholesky.181 = f32[128,128]{1,0:T(8,128)S(1)} custom-call(f32[128,128]{1,0:T(8,128)S(1)} %convolution_subtract_fusion.7), custom_call_target="Cholesky" | custom-call | tf_op jit(solution)/shard_map/jit(cholesky)/cholesky | solution.py:63
  286.5 4.2 %while.10 = (s32[]{:T(128)}, f32[256,256]{1,0:T(8,128)S(1)}, s32[2,2]{1,0:T(2,128)S(1)}, f32[2,128,128]{2,1,0:T(8,128)S(1)}, s32[]{:T(128)}) while((s32[]{:T(128)}, f32[256,256]{1,0:T(8,128)S(1)}, s32[2,2]{1,0:T(2,128)S(1)}, f32[2,128,128]{2,1,0:T(8,128)S(1)}, s32[]{:T(128)}) %tuple.75), condition=%wide.while_cond.clone, body=%wide.while_body.clone.sunk | while | flops 2 | bytes 131181 | solution.py:40
  287.1 1.4 bitcast_dynamic-update-slice_fusion.5
  289.2 1.4 bitcast_dynamic-update-slice_fusion.5
  290.6 20.5 %custom-call.26 = f32[2,128,128]{1,2,0:T(8,128)} custom-call(f32[2,128,128]{2,1,0:T(8,128)S(1)} %get-tuple-element.45), custom_call_target="InvertDiagBlocksLowerTriangular" | custom-call | tf_op jit(solution)/shard_map/triangular_solve/custom-call.0 | solution.py:40
  311.1 2.5 fusion.35
  313.6 2.7 convolution_subtract_fusion
  316.3 2.1 fusion.69
  318.4 1.8 copy.58
  320.2 1.1 broadcast_in_dim.178
  322.5 2.0 pad_maximum_fusion.1
  326.8 2.0 copy.61
  328.8 1.8 copy.88
  330.7 2.2 fusion.21
  332.9 1.0 copy-done.26
  334.5 1.8 convolution_subtract_fusion.4
  337.4 1.6 broadcast_select_fusion.2
  339.0 1.7 copy.87
  340.9 2.2 copy.92
  343.2 1.6 copy.89
  344.8 2.2 convolution_subtract_fusion.2
  347.7 1.8 convolution_subtract_fusion.3
  350.6 1.2 fusion.39
  351.8 2.5 copy.91
  354.3 7.4 %fusion.86 = f32[4,256,8,256]{3,1,2,0:T(8,128)S(1)} fusion(f32[4,256,256,1]{2,1,3,0:T(8,128)S(1)} %bitcast.288, f32[8,256,256,1]{2,1,0,3:T(8,128)S(1)} %bitcast.286), kind=kOutput, calls=%fused_computation.173 | convolution fusion | flops 6442450944 | bytes 11534336 | tf_op jit(solution)/shard_map/aik,bjk->abij/dot_general | solution.py:47
  361.8 7.6 %fusion.87 = f32[4,256,8,256]{3,1,2,0:T(8,128)S(1)} fusion(f32[4,256,256,1]{2,1,3,0:T(8,128)S(1)} %bitcast.289, f32[8,256,256,1]{2,1,0,3:T(8,128)S(1)} %bitcast.287), kind=kOutput, calls=%fused_computation.174 | convolution fusion | flops 6442450944 | bytes 11534336 | tf_op jit(solution)/shard_map/aik,bjk->abij/dot_general | solution.py:47
  369.5 8.5 %fusion.2 = f32[8,1,4,1,256,256]{4,5,0,2,3,1:T(8,128)} fusion(f32[4,256,8,256]{3,1,2,0:T(8,128)S(1)} %fusion.87, f32[4,256,8,256]{3,1,2,0:T(8,128)S(1)} %fusion.86, f32[256,256]{0,1:T(8,128)S(1)} %copy-done.30, f32[8,4]{0,1:T(4,128)S(1)} %copy-done.46, f32[4,256]{1,0:T(4,128)S(1)} %copy-done.39, f32[8,256]{1,0:T(8,128)S(1)} %fusion.7, ...), kind=kOutput, calls=%fused_computation.8 | convolution fusion | flops 2168455168 | bytes 30683276 | tf_op jit(solution)/shard_map/aip,bjp->abij/dot_general | solution.py:23
  378.0 9.1 %copy.75 = f32[8,1,4,1,256,256]{5,4,3,2,1,0:T(8,128)} copy(f32[8,1,4,1,256,256]{4,5,0,2,3,1:T(8,128)} %fusion.2) | data formatting | bytes 16777216 | tf_op jit(solution)/shard_map/reshape | solution.py:134
  (180 shorter events, 29.6 us)
Async XLA Ops:
  6.5 55.0 %all-gather.3.cloned.1.call-start = ((), (), s32[]{:S(2)}) async-start(), calls=%async_computation | async-start | bytes 2359296 | tf_op jit(solution)/shard_map/all_gather | solution.py:88
  7.3 117.1 %all-reduce.3.cloned.1.call-start = ((), (), s32[]{:S(2)}) async-start(), calls=%async_computation.2 | async-start | bytes 2097152 | tf_op jit(solution)/shard_map/psum | solution.py:12
  8.7 81.7 %copy-start.42 = (pred[8]{0:T(512)(128)(4,1)}, pred[8]{0:T(512)(128)(4,1)S(1)}, u32[]{:S(2)}) copy-start(pred[8]{0:T(512)(128)(4,1)S(1)} %broadcast_compare_fusion.4) | copy-start | bytes 28
  9.3 81.1 %copy-start.44 = (pred[8]{0:T(512)(128)(4,1)}, pred[8]{0:T(512)(128)(4,1)S(1)}, u32[]{:S(2)}) copy-start(pred[8]{0:T(512)(128)(4,1)S(1)} %get-tuple-element.99) | copy-start | bytes 28
  9.4 136.2 %copy-start.29 = (f32[256,256]{0,1:T(8,128)}, f32[256,256]{0,1:T(8,128)S(1)}, u32[]{:S(2)}) copy-start(f32[256,256]{0,1:T(8,128)S(1)} %fusion.59) | copy-start | bytes 786436
  88.0 3.9 copy-start.37
  89.4 53.7 %all-gather.5.cloned.1.call-start = ((), (), s32[]{:S(2)}) async-start(), calls=%async_computation.1 | async-start | bytes 1310720 | tf_op jit(solution)/shard_map/all_gather | solution.py:106
  93.9 1.3 copy-start
  124.3 2.6 copy-start.14
  125.8 1.1 copy-start.15
  143.1 2.5 copy-start.28
  145.6 1.5 copy-start.41
  146.2 53.8 %copy-start.27 = (f32[2,2,256,256]{2,3,1,0:T(8,128)}, f32[2,2,256,256]{2,3,1,0:T(8,128)S(1)}, u32[]{:S(2)}) copy-start(f32[2,2,256,256]{2,3,1,0:T(8,128)S(1)} %fusion.30) | copy-start | bytes 3145732
  147.1 78.0 %copy-start.3 = (bf16[8,256,512]{2,1,0:T(8,128)(2,1)S(1)}, bf16[8,256,512]{2,1,0:T(8,128)(2,1)}, u32[]{:S(2)}) copy-start(bf16[8,256,512]{2,1,0:T(8,128)(2,1)} %get-tuple-element.64) | copy-start | bytes 6291460
  148.4 0.7 copy-start.34
  195.7 2.6 copy-start.32
  204.9 0.6 copy-start.47
  205.5 25.9 %copy-start.19 = (f32[256,256]{1,0:T(8,128)}, f32[256,256]{1,0:T(8,128)S(1)}, u32[]{:S(2)}) copy-start(f32[256,256]{1,0:T(8,128)S(1)} %get-tuple-element.195) | copy-start | bytes 786436
  225.2 8.1 %copy-start.24 = (f32[2,128,128]{1,2,0:T(8,128)}, f32[2,128,128]{1,2,0:T(8,128)S(1)}, u32[]{:S(2)}) copy-start(f32[2,128,128]{1,2,0:T(8,128)S(1)} %custom-call.24) | copy-start | bytes 393220
  228.3 2.0 copy-start.11
  231.4 3.9 copy-start.33
  235.6 0.9 copy-start.25
  235.6 1.0 copy-start.31
  235.7 5.1 %copy-start.13 = (f32[2048,128]{0,1:T(8,128)S(1)}, f32[2048,128]{0,1:T(8,128)}, u32[]{:S(2)}) copy-start(f32[2048,128]{0,1:T(8,128)} %fusion.74) | copy-start | bytes 3145732
  238.4 4.1 %copy-start.21 = (f32[256,128]{0,1:T(8,128)}, f32[256,128]{0,1:T(8,128)S(1)}, u32[]{:S(2)}) copy-start(f32[256,128]{0,1:T(8,128)S(1)} %fusion.73) | copy-start | bytes 393220
  240.7 2.9 copy-start.12
  243.7 5.2 %copy-start.18 = (f32[256,256]{0,1:T(8,128)S(1)}, f32[256,256]{0,1:T(8,128)}, u32[]{:S(2)}) copy-start(f32[256,256]{0,1:T(8,128)} %convolution_subtract_fusion.5) | copy-start | bytes 786436
  248.8 37.6 %copy-start.48 = (s32[2,2]{1,0:T(2,128)S(1)}, s32[2,2]{1,0:T(2,128)}, u32[]{:S(2)}) copy-start(s32[2,2]{1,0:T(2,128)} %copy-done.47) | copy-start | bytes 52
  290.6 20.5 %copy-start.23 = (f32[256,256]{1,0:T(8,128)}, f32[256,256]{1,0:T(8,128)S(1)}, u32[]{:S(2)}) copy-start(f32[256,256]{1,0:T(8,128)S(1)} %get-tuple-element.196) | copy-start | bytes 786436
  311.1 2.5 copy-start.1
  313.6 2.7 copy-start.35
  321.3 1.2 copy-start.17
  321.3 1.2 copy-start.38
  325.3 1.0 copy-start.9
  325.3 0.9 copy-start.43
  325.3 0.9 copy-start.45
  326.8 2.0 copy-start.2
  328.8 1.8 copy-start.16
  328.8 1.8 copy-start.39
  332.8 3.6 copy-start.20
  332.8 1.0 copy-start.26
  339.0 1.9 copy-start.5
  343.2 1.6 copy-start.22
  344.8 2.3 copy-start.36
  347.0 3.1 copy-start.10
  349.5 1.0 copy-start.40
  350.6 3.7 copy-start.6
  354.3 7.4 %copy-start.7 = (f32[2048,256]{1,0:T(8,128)S(1)}, f32[2048,256]{1,0:T(8,128)}, u32[]{:S(2)}) copy-start(f32[2048,256]{1,0:T(8,128)} %copy.92) | copy-start | bytes 6291460
  354.3 7.4 %copy-start.8 = (f32[1024,256]{1,0:T(8,128)S(1)}, f32[1024,256]{1,0:T(8,128)}, u32[]{:S(2)}) copy-start(f32[1024,256]{1,0:T(8,128)} %copy.91) | copy-start | bytes 3145732
  361.8 7.7 %copy-start.4 = (bf16[8,256,512]{2,1,0:T(8,128)(2,1)S(1)}, bf16[8,256,512]{2,1,0:T(8,128)(2,1)}, u32[]{:S(2)}) copy-start(bf16[8,256,512]{2,1,0:T(8,128)(2,1)} %get-tuple-element.64) | copy-start | bytes 6291460
  361.8 7.7 %copy-start.30 = (f32[256,256]{0,1:T(8,128)S(1)}, f32[256,256]{0,1:T(8,128)}, u32[]{:S(2)}) copy-start(f32[256,256]{0,1:T(8,128)} %copy-done.29) | copy-start | bytes 786436
  361.8 7.7 %copy-start.46 = (f32[8,4]{0,1:T(4,128)S(1)}, f32[8,4]{0,1:T(4,128)}, u32[]{:S(2)}) copy-start(f32[8,4]{0,1:T(4,128)} %compare_select_fusion.4) | copy-start | bytes 388
  361.8 7.7 %copy-start.49 = (pred[8]{0:T(512)(128)(4,1)S(1)}, pred[8]{0:T(512)(128)(4,1)}, u32[]{:S(2)}) copy-start(pred[8]{0:T(512)(128)(4,1)} %get-tuple-element.98) | copy-start | bytes 28
  361.8 7.7 %copy-start.50 = (pred[4]{0:T(512)(128)(4,1)S(1)}, pred[4]{0:T(512)(128)(4,1)}, u32[]{:S(2)}) copy-start(pred[4]{0:T(512)(128)(4,1)} %broadcast_compare_fusion.5) | copy-start | bytes 16
Sparse Core Ops, SparseCore 0:
  9.5 51.9 all-gather.2
  89.6 34.7 all-reduce.2
  126.0 17.0 all-gather.4
where the time goes:
time: 393 us; the launch traced here: 394 us
  other arithmetic  147 us (37%)
  waiting for transfers between devices  89.7 us (23%)
  local copies, waits for them, and re-layouts  78 us (20%)
  matrix products  61.9 us (16%)
  between operations  17 us (4%)
    all_gather x1, waiting for transfers between devices, per_device(): gathered = lax.all_gather(gradients, 'col', axis=2, tiled=True)  50.7 us
    another operation x6, other arithmetic, lead_factors(): lower_first = jnp.linalg.cholesky(corner[0, 0])  45.7 us
    another operation x6, other arithmetic, right_solve(): lax.linalg.triangular_solve(factor, stacked, left_side=False, lower=True,...  45.1 us
    another operation x7, other arithmetic, lead_factors(): return (lower_first, below_factor, jnp.linalg.cholesky(reduced))  34.7 us
    gather x1, local copies, waits for them, and re-layouts, per_device(): own_rows = jnp.take_along_axis(stacked, slot_ids[:, :, None], axis=1)  26.4 us
    psum x1, waiting for transfers between devices, broadcast(): return lax.psum(kept, axis)  23 us
    another operation x15, matrix products, right_solve(): lax.linalg.triangular_solve(factor, stacked, left_side=False, lower=True,...  20.1 us
    all_gather x1, waiting for transfers between devices, per_device(): leaders = lax.all_gather(own_rows[:1], 'row', axis=0, tiled=True)[:2]  15.2 us
  transfers between devices with their start and end apart: 3, of which 3 were waited for; matrix products, arithmetic and copies ran while one was open for 4% of the time, Pallas kernels for 0%

commit v1 on v0

v1 whole, which is shorter than its diff:
```python
import functools

import jax
import jax.numpy as jnp
from jax import lax
from jax.experimental import pallas as pl
from jax.experimental.pallas import tpu as pltpu
from jax.sharding import PartitionSpec as P

RIDGE = 0.5
F32 = jnp.float32
BF16 = jnp.bfloat16


def mm(a, b):
    return jnp.dot(a, b, preferred_element_type=F32)


def mm_nt(a, b):
    return lax.dot_general(a, b, (((1,), (1,)), ((), ())), preferred_element_type=F32)


def mm_tn(a, b):
    return lax.dot_general(a, b, (((0,), (0,)), ((), ())), preferred_element_type=F32)


def split(x):
    high = x.astype(BF16)
    return high, (x - high.astype(F32)).astype(BF16)


def mm3(product, a, b):
    a_high, a_low = a
    b_high, b_low = b
    return product(a_high, b_high) + (product(a_high, b_low) + product(a_low, b_high))


def ordered(raw, order_row):
    size = raw.shape[0]
    source = lax.broadcasted_iota(jnp.int32, (size, size), 0)
    chosen = jnp.where(source == order_row, 1.0, 0.0).astype(BF16)
    return mm_tn(chosen, raw).astype(BF16)


def scale(cand, weights):
    widened = cand.astype(F32)
    scaled = (widened * weights).astype(BF16)
    return scaled, jnp.sum(scaled.astype(F32) * widened, axis=1, keepdims=True)


def as_row(column):
    size = column.shape[0]
    return jnp.transpose(jnp.broadcast_to(column, (size, 128)))[0:8, :]


def tile(scaled, squares, cand, squares_row):
    return jnp.exp(-0.5 * (squares + squares_row - 2.0 * mm_nt(scaled, cand)))


def eye(size):
    rows = lax.broadcasted_iota(jnp.int32, (size, size), 0)
    return rows == lax.broadcasted_iota(jnp.int32, (size, size), 1)


STRIP = 128
MICRO = 8


def factor_strip(work):
    sub = lax.broadcasted_iota(jnp.int32, (MICRO, 128), 0)
    for step in range(STRIP // MICRO):
        base = step * MICRO
        rows = work[base : base + MICRO, :]
        left, right = rows[:, :128], rows[:, 128:]
        lanes = [
            jnp.broadcast_to(left[:, base + j : base + j + 1], (MICRO, 128)) for j in range(MICRO)
        ]
        for k in range(MICRO):
            pivot = lax.rsqrt(jnp.broadcast_to(lanes[k][k : k + 1, :], (MICRO, 128)))
            factor = lanes[k] * pivot
            below = jnp.where(sub > k, factor, 0.0)
            for j in range(k + 1, MICRO):
                lanes[j] = lanes[j] - below * jnp.broadcast_to(factor[j : j + 1, :], (MICRO, 128))
            left_k = left * pivot
            right_k = right * pivot
            left = jnp.where(
                sub == k, left_k, left - below * jnp.broadcast_to(left_k[k : k + 1], (MICRO, 128))
            )
            right = jnp.where(
                sub == k, right_k, right - below * jnp.broadcast_to(right_k[k : k + 1], (MICRO, 128))
            )
        done = jnp.concatenate([left, right], axis=1)
        work[base : base + MICRO, :] = done
        if base + MICRO < STRIP:
            high = done.astype(BF16).astype(F32)
            low = done - high
            rhs = jnp.concatenate([high, low, high], axis=0).astype(BF16)
            left_high, left_low = high[:, :128], low[:, :128]
            lhs = jnp.concatenate(
                [left_high, left_high, left_low, jnp.zeros((128 - 3 * MICRO, 128), F32)], axis=0
            )
            turned = jnp.transpose(lhs)[base + MICRO :, : 3 * MICRO].astype(BF16)
            work[base + MICRO :, :] = work[base + MICRO :, :] - mm(turned, rhs)


def corner_kernel(raw, order, weights, cand_out, squares_out, lower_out, inv_high, inv_low,
                  corner, upper, inverse, work):
    size = raw.shape[1]
    cands, scaleds, squares = [], [], []
    for block in range(2):
        cand = ordered(raw[block], order[block : block + 1, :])
        scaled, square = scale(cand, weights[...])
        cand_out[block * size : (block + 1) * size, :] = cand
        squares_out[:, block * size : (block + 1) * size] = as_row(square)
        cands.append(cand)
        scaleds.append(scaled)
        squares.append(square)
    for block in range(2):
        own = slice(block * size, (block + 1) * size)
        square = tile(scaleds[block], squares[block], cands[block], squares_out[0:1, own])
        square = 0.5 * (square + jnp.transpose(square))
        corner[own, own] = square + jnp.where(eye(size), RIDGE, 0.0)
    cross = tile(scaleds[1], squares[1], cands[0], squares_out[0:1, :size])
    corner[:size, size:] = jnp.transpose(cross)
    corner[size:, :size] = cross
    upper[...] = jnp.zeros_like(upper)
    inverse[...] = jnp.zeros_like(inverse)

    def strip(index, _):
        own = pl.ds(pl.multiple_of(index * STRIP, STRIP), STRIP)
        left = split(jnp.transpose(upper[:, own]))
        current = corner[own, :] - mm3(mm, left, split(upper[...]))
        inverse_part = mm3(mm, left, split(inverse[...]))
        corner[own, :] = current
        work[:, :STRIP] = corner[own, own]
        work[:, STRIP:] = jnp.where(eye(STRIP), 1.0, 0.0)
        factor_strip(work)
        diagonal_inverse = work[:, STRIP:]
        turn = split(diagonal_inverse)
        rows = mm3(mm, turn, split(current))
        column = lax.broadcasted_iota(jnp.int32, rows.shape, 1)
        row = lax.broadcasted_iota(jnp.int32, rows.shape, 0) + index * STRIP
        upper[own, :] = jnp.where(column >= row, rows, 0.0)
        inverse[own, :] = -mm3(mm, turn, split(inverse_part))
        inverse[own, own] = diagonal_inverse
        return 0

    lax.fori_loop(0, corner.shape[0] // STRIP, strip, 0)
    lower_out[...] = jnp.transpose(upper[...])
    high, low = split(inverse[...])
    inv_high[...] = high
    inv_low[...] = low


def corner_call(raw, order, weights):
    size, features = raw.shape[1:]
    whole = 2 * size
    return pl.pallas_call(
        corner_kernel,
        out_shape=(
            jax.ShapeDtypeStruct((whole, features), BF16),
            jax.ShapeDtypeStruct((8, whole), F32),
            jax.ShapeDtypeStruct((whole, whole), F32),
            jax.ShapeDtypeStruct((whole, whole), BF16),
            jax.ShapeDtypeStruct((whole, whole), BF16),
        ),
        scratch_shapes=[
            pltpu.VMEM((whole, whole), F32),
            pltpu.VMEM((whole, whole), F32),
            pltpu.VMEM((whole, whole), F32),
            pltpu.VMEM((STRIP, 2 * STRIP), F32),
        ],
        compiler_params=pltpu.CompilerParams(vmem_limit_bytes=24 << 20),
        cost_estimate=pl.CostEstimate(
            flops=20_000_000_000, bytes_accessed=4 << 20, transcendentals=0
        ),
        name="corner",
    )(raw, order, weights)


def window_kernel(row_count, col_count, place, rows_raw, rows_order, cols_raw, cols_order, weights,
                  lead, lead_squares, lower, inv_high, inv_low, out,
                  col_cand, col_squares, col_high, col_low):
    step = pl.program_id(0)
    row_index, col_index = place[0], place[1]
    size = rows_raw.shape[1]
    local_cols = cols_raw.shape[0]
    label = step * row_count + row_index

    def panel(scaled, squares, block):
        entries = tile(scaled, squares, lead[...], lead_squares[0:1, :])
        inverse = (inv_high[...], inv_low[...])
        solved = mm3(mm_nt, split(entries), inverse)
        start = pl.multiple_of(jnp.minimum(block, 1) * size, size)
        return jnp.where(block < 2, lower[pl.ds(start, size), :], solved)

    @pl.when(step == 0)
    def _():
        for b in range(local_cols):
            own = slice(b * size, (b + 1) * size)
            cand = ordered(cols_raw[b], cols_order[b : b + 1, :])
            scaled, squares = scale(cand, weights[...])
            high, low = split(panel(scaled, squares, b * col_count + col_index))
            col_cand[own, :] = cand
            col_squares[:, own] = as_row(squares)
            col_high[own, :] = high
            col_low[own, :] = low

    cand = ordered(rows_raw[0], rows_order[pl.ds(step, 1), :])
    scaled, squares = scale(cand, weights[...])
    factors = panel(scaled, squares, label)
    halves = split(factors)
    for b in range(local_cols):
        own = slice(b * size, (b + 1) * size)
        column = b * col_count + col_index
        entries = tile(scaled, squares, col_cand[own, :], col_squares[0:1, own])
        entries = entries - mm3(mm_nt, halves, (col_high[own, :], col_low[own, :]))
        ridge = jnp.where(label == column, RIDGE, 0.0)
        entries = entries + jnp.where(eye(size), ridge, 0.0)
        entries = jnp.where(label < 2, 0.0, entries)
        if b == 0:
            lead_part = jnp.where(column == 0, factors[:, :size], factors[:, size:])
            entries = jnp.where(column < 2, lead_part, entries)
        out[0, 0, b, 0] = entries


def window_call(row_count, col_count, place, rows_raw, rows_order, cols_raw, cols_order, weights,
                corner):
    local_rows, size, features = rows_raw.shape
    local_cols = cols_raw.shape[0]
    whole = 2 * size

    def fixed(shape):
        return pl.BlockSpec(shape, lambda i, *_: (0,) * len(shape))

    return pl.pallas_call(
        functools.partial(window_kernel, row_count, col_count),
        out_shape=jax.ShapeDtypeStruct((local_rows, 1, local_cols, 1, size, size), F32),
        grid=(local_rows,),
        in_specs=[
            pl.BlockSpec(memory_space=pltpu.SMEM),
            pl.BlockSpec((1, size, features), lambda i: (i, 0, 0)),
            fixed((local_rows, size)),
            fixed((local_cols, size, features)),
            fixed((local_cols, size)),
            fixed((1, features)),
            fixed((whole, features)),
            fixed((8, whole)),
            fixed((whole, whole)),
            fixed((whole, whole)),
            fixed((whole, whole)),
        ],
        out_specs=pl.BlockSpec(
            (1, 1, local_cols, 1, size, size), lambda i: (i, 0, 0, 0, 0, 0)
        ),
        scratch_shapes=[
            pltpu.VMEM((local_cols * size, features), BF16),
            pltpu.VMEM((8, local_cols * size), F32),
            pltpu.VMEM((local_cols * size, whole), BF16),
            pltpu.VMEM((local_cols * size, whole), BF16),
        ],
        compiler_params=pltpu.CompilerParams(vmem_limit_bytes=40 << 20),
        name="window",
    )(place, rows_raw, rows_order, cols_raw, cols_order, weights, *corner)


def per_device(gradients, feature_weights, order):
    row_count = lax.axis_size("row")
    col_count = lax.axis_size("col")
    row_index = lax.axis_index("row")
    col_index = lax.axis_index("col")
    ratio = col_count // row_count
    local_rows, _, _, part, features = gradients.shape
    size = order.shape[2]
    weights = feature_weights.reshape(1, features)
    orders = lax.all_gather(order, "row", axis=1, tiled=True)
    leaders = lax.all_gather(gradients[0, 0], ("row", "col"), axis=0, tiled=False)
    leaders = leaders.reshape(row_count, size, features)[:2]
    gathered = lax.all_gather(gradients, "col", axis=2, tiled=True)
    rows_raw = gathered.reshape(local_rows, size, features)
    source = col_index % row_count

    def pick(blocks):
        grouped = blocks.reshape((local_rows // ratio, ratio) + blocks.shape[1:])
        return lax.dynamic_index_in_dim(grouped, col_index // row_count, axis=1, keepdims=False)

    kept = jnp.where(row_index == source, pick(rows_raw), 0).astype(BF16)
    cols_raw = lax.psum(kept, "row")
    cols_order = pick(lax.dynamic_index_in_dim(orders, source, axis=1, keepdims=False))
    corner = corner_call(leaders, orders[0, :2], weights)
    place = jnp.stack([row_index, col_index]).astype(jnp.int32)
    return window_call(
        row_count, col_count, place, rows_raw, order.reshape(local_rows, size), cols_raw,
        cols_order, weights, corner,
    )


def solution(mesh):
    placed = (P(None, "row", "col", None, None), P(), P(None, "row", None))
    return jax.shard_map(
        per_device,
        mesh=mesh,
        in_specs=placed,
        out_specs=P(None, "row", None, "col", None, None),
        check_vma=False,
    )
```

time: 393 us -> 189 us (0.48)
  other arithmetic: 147 us -> 2.34 us
  local copies, waits for them, and re-layouts: 78 us -> 11.8 us
  matrix products: 61.9 us -> 0 us
  Pallas kernels: 0 us -> 52.3 us
  waiting for transfers between devices: 89.7 us -> 103 us
  blocking collectives: 0 us -> 6.16 us
    another operation x19 -> x1, other arithmetic: 126 us -> 0.08 us  [per_device(): place = jnp.stack([row_index, col_index]).astype(jnp.int32)]
    pallas_call x0 -> x2, Pallas kernels: none -> 52.3 us  [the longest x1 29.1 us: corner_call(): pl.pallas_call(corner_kernel, out_shape=(jax.ShapeDtypeStruct((whole, fea...]
    dot_general x9 -> x0, matrix products: 39.2 us -> none  [the longest x2 15 us: outer_update(): jnp.einsum('aik,bjk->abij', row_factors, col_factors, precision=EXACT)]
    all_gather x1, waiting for transfers between devices: 15.2 us -> 51.2 us  [per_device(): lax.all_gather(gradients[0, 0], ('row', 'col'), axis=0, tiled=False)]
    gather x1 -> x0, local copies, waits for them, and re-layouts: 26.4 us -> none  [per_device(): own_rows = jnp.take_along_axis(stacked, slot_ids[:, :, None], axis=1)]
    another operation x19 -> x0, matrix products: 22.7 us -> none  [the longest x15 20.1 us: right_solve(): lax.linalg.triangular_solve(factor, stacked, left_side=False, lower=True,...]
    psum x1, waiting for transfers between devices: 23 us -> 2.58 us  [per_device(): cols_raw = lax.psum(kept, 'row')]
    select_n x7 -> x0, local copies, waits for them, and re-layouts: 12.3 us -> none  [the longest x2 4.78 us: panel_pair(): second_panel = jnp.where((labels == 0)[:, None, None], 0.0, second_panel)]
  transfers between devices with their start and end apart: 3 -> 3, of which waited for: 3 -> 3; matrix products, arithmetic and copies ran while one was open for 4% -> 1% of each run, Pallas kernels for 0% -> 15%
where the time goes in v1:
time: 189 us
  waiting for transfers between devices  103 us (54%)
  Pallas kernels  52.3 us (28%)
  between operations  13.2 us (7%)
  local copies, waits for them, and re-layouts  11.8 us (6%)
  blocking collectives  6.16 us (3%)
  other arithmetic  2.34 us (1%)
    all_gather x1, waiting for transfers between devices, per_device(): lax.all_gather(gradients[0, 0], ('row', 'col'), axis=0, tiled=False)  51.2 us
    all_gather x1, waiting for transfers between devices, per_device(): gathered = lax.all_gather(gradients, 'col', axis=2, tiled=True)  48.5 us
    pallas_call x1, Pallas kernels, corner_call(): pl.pallas_call(corner_kernel, out_shape=(jax.ShapeDtypeStruct((whole, fea...  29.1 us
    pallas_call x1, Pallas kernels, window_call(): pl.pallas_call(functools.partial(window_kernel, row_count, col_count), ou...  23.2 us
    unnamed x23, local copies, waits for them, and re-layouts  8.48 us
    all_gather x1, blocking collectives, per_device(): orders = lax.all_gather(order, 'row', axis=1, tiled=True)  6.16 us
  transfers between devices with their start and end apart: 3, of which 3 were waited for; matrix products, arithmetic and copies ran while one was open for 1% of the time, Pallas kernels for 15%

profile of v1, /device:TPU:0, one launch (start us, length us, event | category | flops | bytes accessed | tf_op | source)
XLA Modules:
  0.0 188.8 jit_solution(11363941777573697933)
XLA Ops:
  6.5 0.0 all-gather.6.cloned.1.call-start
  6.5 1.4 slice.12
  7.9 0.0 all-gather.6.cloned.1.call-update
  7.9 0.0 all-gather.4.cloned.1.call-start
  8.0 0.7 all-gather.4.cloned.1.call-update
  8.7 0.0 all-reduce.2.cloned.1.call-start
  8.8 0.7 copy.20
  9.5 6.2 %all_gather.10 = s32[8,4,256]{2,0,1:T(8,128)S(1)} all-gather(s32[8,1,256]{2,0,1:T(8,128)S(1)} %copy.20), channel_id=1, replica_groups=mesh['row'=4,'col'=8] {'row'}, dimensions={1}, use_global_device_ids=true | all-gather | bytes 40960 | tf_op jit(solution)/shard_map/all_gather | solution.py:276
  15.7 0.1 pad_add_fusion.place
  15.8 0.0 copy-start.9
  15.8 51.2 %all-gather.6.cloned.1.call-done = bf16[32,1,1,32,512]{4,3,2,1,0:T(8,128)(2,1)} async-done(((bf16[1,1,1,32,512]{4,3,2,1,0:T(8,128)(2,1)}), bf16[32,1,1,32,512]{4,3,2,1,0:T(8,128)(2,1)}) %all-gather.6.cloned.1.call-update) | async-done | bytes 1048592 | tf_op jit(solution)/shard_map/all_gather | solution.py:277
  67.0 1.9 slice.17
  68.9 48.5 %all-gather.4.cloned.1.call-done = bf16[8,1,8,32,512]{4,3,2,0,1:T(8,128)(2,1)} async-done(((bf16[8,1,1,32,512]{4,3,2,0,1:T(8,128)(2,1)}), bf16[8,1,8,32,512]{4,3,2,0,1:T(8,128)(2,1)}) %all-gather.4.cloned.1.call-update) | async-done | bytes 2097168 | tf_op jit(solution)/shard_map/all_gather | solution.py:279
  117.3 2.3 %fusion = bf16[4,256,512]{2,1,0:T(8,128)(2,1)} fusion(bf16[4,2,256,512]{3,2,1,0:T(8,128)(2,1)} %bitcast.23, s32[]{:T(128)S(6)} %select_n.36, pred[]{:T(512)S(6)} %eq.5), kind=kLoop, calls=%fused_computation.1 | loop fusion | flops 524288 | bytes 2097157 | tf_op jit(solution)/shard_map/jit(_where)/select_n | solution.py:287
  119.6 0.0 all-reduce.2.cloned.1.call-update
  119.6 0.0 copy-done.9
  119.6 0.0 copy-start.2
  119.6 1.0 copy-done.2
  120.7 0.0 copy-start
  120.7 29.1 %corner.1 = (bf16[512,512]{1,0:T(8,128)(2,1)S(1)}, f32[8,512]{1,0:T(8,128)S(1)}, f32[512,512]{1,0:T(8,128)S(1)}, bf16[512,512]{1,0:T(8,128)(2,1)S(1)}, bf16[512,512]{1,0:T(8,128)(2,1)S(1)}) custom-call(bf16[2,256,512]{2,1,0:T(8,128)(2,1)S(1)} %bitcast.25, s32[2,256]{1,0:T(2,128)S(1)} %bitcast.30, f32[1,512]{1,0:T(1,128)S(1)} %bitcast.28), custom_call_target="tpu_custom_call" | custom-call | flops 20000000000 | bytes 4194304 | tf_op jit(solution)/shard_map/corner/pallas_call | solution.py:158
  149.8 0.0 copy-start.3
  149.8 0.8 copy-done.3
  150.6 0.0 copy-start.5
  150.6 0.8 copy-done.5
  151.4 0.0 copy-start.7
  151.4 0.8 copy-done.7
  152.2 2.6 %all-reduce.2.cloned.1.call-done.cols_raw = bf16[4,256,512]{2,1,0:T(8,128)(2,1)} async-done(((bf16[4,256,512]{2,1,0:T(8,128)(2,1)}), bf16[4,256,512]{2,1,0:T(8,128)(2,1)}) %all-reduce.2.cloned.1.call-update) | async-done | bytes 1048592 | tf_op jit(solution)/shard_map/psum | solution.py:288
  154.7 0.0 copy-done
  154.8 0.0 copy-start.1
  154.8 1.2 copy-done.1
  156.0 0.0 copy-start.4
  156.0 1.0 copy-done.4
  157.0 0.0 copy-start.6
  157.0 1.0 copy-done.6
  158.1 0.0 copy-start.8
  158.1 1.0 copy-done.8
  159.1 23.2 %window.1 = f32[8,1,4,1,256,256]{5,4,3,2,1,0:T(8,128)} custom-call(s32[2]{0:T(128)S(1)} %pad_add_fusion.place, bf16[8,256,512]{2,1,0:T(8,128)(2,1)S(1)} %bitcast.24, s32[8,256]{1,0:T(8,128)S(1)} %bitcast.26, bf16[4,256,512]{2,1,0:T(8,128)(2,1)S(1)} %copy-done.1, s32[4,256]{1,0:T(4,128)S(1)} %bitcast.27, f32[1,512]{1,0:T(1,128)S(1)} %bitcast.29, ...), custom_call_target="tpu_custom_call" | custom-call | tf_op jit(solution)/shard_map/window/pallas_call | solution.py:236
  (6 shorter events, 0.0 us)
Async XLA Ops:
  6.5 60.4 %all-gather.6.cloned.1.call-start = ((), (), s32[]{:S(2)}) async-start(), calls=%async_computation.2 | async-start | bytes 1081344 | tf_op jit(solution)/shard_map/all_gather | solution.py:277
  7.9 109.4 %all-gather.4.cloned.1.call-start = ((), (), s32[]{:S(2)}) async-start(), calls=%async_computation | async-start | bytes 2359296 | tf_op jit(solution)/shard_map/all_gather | solution.py:279
  8.7 146.1 %all-reduce.2.cloned.1.call-start = ((), (), s32[]{:S(2)}) async-start(), calls=%async_computation.1 | async-start | bytes 2097152 | tf_op jit(solution)/shard_map/psum | solution.py:288
  15.8 103.9 %copy-start.9 = (f32[512]{0:T(512)S(1)}, f32[512]{0:T(512)}, u32[]{:S(2)}) copy-start(f32[512]{0:T(512)} %param.4) | copy-start | bytes 6148
  119.6 1.0 copy-start.2
  120.7 34.1 %copy-start = (bf16[8,1,8,32,512]{4,3,2,0,1:T(8,128)(2,1)S(1)}, bf16[8,1,8,32,512]{4,3,2,0,1:T(8,128)(2,1)}, u32[]{:S(2)}) copy-start(bf16[8,1,8,32,512]{4,3,2,0,1:T(8,128)(2,1)} %all-gather.4.cloned.1.call-done) | copy-start | bytes 6291460
  149.8 0.8 copy-start.3
  150.6 0.8 copy-start.5
  151.4 0.8 copy-start.7
  154.8 1.2 copy-start.1
  156.0 1.0 copy-start.4
  157.0 1.0 copy-start.6
  158.1 1.0 copy-start.8
Sparse Core Ops, SparseCore 0:
  10.4 56.5 all-gather.5
  69.2 48.1 all-gather.3
  119.7 34.9 all-reduce.1

commit v2 on v1

--- a/solution.py
+++ b/solution.py
@@ -108,7 +108,7 @@
     size = raw.shape[1]
     cands, scaleds, squares = [], [], []
     for block in range(2):
-        cand = ordered(raw[block], order[block : block + 1, :])
+        cand = ordered(raw[block], order[block, 0:1, :])
         scaled, square = scale(cand, weights[...])
         cand_out[block * size : (block + 1) * size, :] = cand
         squares_out[:, block * size : (block + 1) * size] = as_row(square)
@@ -178,11 +178,13 @@
     )(raw, order, weights)
 
 
-def window_kernel(row_count, col_count, place, rows_raw, rows_order, cols_raw, cols_order, weights,
+def window_kernel(row_count, col_count, rows_raw, orders, cols_raw, weights,
                   lead, lead_squares, lower, inv_high, inv_low, out,
                   col_cand, col_squares, col_high, col_low):
     step = pl.program_id(0)
-    row_index, col_index = place[0], place[1]
+    row_index, col_index = lax.axis_index("row"), lax.axis_index("col")
+    ratio = col_count // row_count
+    source, group = lax.rem(col_index, row_count), lax.div(col_index, row_count)
     size = rows_raw.shape[1]
     local_cols = cols_raw.shape[0]
     label = step * row_count + row_index
@@ -198,7 +200,7 @@
     def _():
         for b in range(local_cols):
             own = slice(b * size, (b + 1) * size)
-            cand = ordered(cols_raw[b], cols_order[b : b + 1, :])
+            cand = ordered(cols_raw[b], orders[source, pl.ds(b * ratio + group, 1), :])
             scaled, squares = scale(cand, weights[...])
             high, low = split(panel(scaled, squares, b * col_count + col_index))
             col_cand[own, :] = cand
@@ -206,7 +208,7 @@
             col_high[own, :] = high
             col_low[own, :] = low
 
-    cand = ordered(rows_raw[0], rows_order[pl.ds(step, 1), :])
+    cand = ordered(rows_raw[0], orders[row_index, pl.ds(step, 1), :])
     scaled, squares = scale(cand, weights[...])
     factors = panel(scaled, squares, label)
     halves = split(factors)
@@ -224,8 +226,7 @@
         out[0, 0, b, 0] = entries
 
 
-def window_call(row_count, col_count, place, rows_raw, rows_order, cols_raw, cols_order, weights,
-                corner):
+def window_call(row_count, col_count, rows_raw, orders, cols_raw, weights, corner):
     local_rows, size, features = rows_raw.shape
     local_cols = cols_raw.shape[0]
     whole = 2 * size
@@ -238,11 +239,9 @@
         out_shape=jax.ShapeDtypeStruct((local_rows, 1, local_cols, 1, size, size), F32),
         grid=(local_rows,),
         in_specs=[
-            pl.BlockSpec(memory_space=pltpu.SMEM),
             pl.BlockSpec((1, size, features), lambda i: (i, 0, 0)),
-            fixed((local_rows, size)),
+            fixed((row_count, local_rows, size)),
             fixed((local_cols, size, features)),
-            fixed((local_cols, size)),
             fixed((1, features)),
             fixed((whole, features)),
             fixed((8, whole)),
@@ -261,37 +260,202 @@
         ],
         compiler_params=pltpu.CompilerParams(vmem_limit_bytes=40 << 20),
         name="window",
-    )(place, rows_raw, rows_order, cols_raw, cols_order, weights, *corner)
+    )(rows_raw, orders, cols_raw, weights, *corner)
+
+
+MESH = pl.DeviceIdType.MESH
+
+
+def gather_kernel(row_count, col_count, grads, order, rows, cols, leads, orders,
+                  lead_send, rows_send, cols_send, order_send,
+                  lead_recv, rows_recv, cols_recv, order_recv, local):
+    row, col = lax.axis_index("row"), lax.axis_index("col")
+    y_count = max(row_count // 2, 1)
+    z_count = col_count // y_count
+    z, y = lax.div(col, y_count), lax.rem(col, y_count)
+    owner = row == lax.rem(col, row_count)
+    group = lax.div(col, row_count)
+    steps = (
+        (z < z_count - 1, col + y_count),
+        (z > 0, col - y_count),
+        (y < y_count - 1, col + 1),
+        (y > 0, col - 1),
+    )
+    others = [lax.rem(row + k, row_count) for k in range(1, row_count)]
+
+    barrier = pltpu.get_barrier_semaphore()
+    expected = row_count - 1
+    for other in others:
+        pl.semaphore_signal(barrier, inc=1, device_id=(other, col), device_id_type=MESH)
+    for inside, neighbour in steps:
+        @pl.when(inside)
+        def _():
+            pl.semaphore_signal(barrier, inc=1, device_id=(row, neighbour), device_id_type=MESH)
+
+        expected = expected + jnp.where(inside, 1, 0)
+    pl.semaphore_wait(barrier, expected)
+
+    started = []
+
+    def push(condition, source, target, send, receive, device):
+        def copy():
+            return pltpu.make_async_remote_copy(
+                src_ref=source, dst_ref=target, send_sem=send, recv_sem=receive,
+                device_id=device, device_id_type=MESH,
+            )
+
+        @pl.when(condition)
+        def _():
+            copy().start()
+
+        started.append((condition, lambda: copy().wait_send()))
+
+    def keep(condition, source, target, sem):
+        def copy():
+            return pltpu.make_async_copy(source, target, sem)
+
+        @pl.when(condition)
+        def _():
+            copy().start()
+
+        started.append((condition, lambda: copy().wait()))
+
+    def arrived(condition, target, receive):
+        @pl.when(condition)
+        def _():
+            pltpu.make_async_remote_copy(
+                src_ref=target, dst_ref=target, send_sem=receive, recv_sem=receive,
+                device_id=(row, col), device_id_type=MESH,
+            ).wait_recv()
+
+    def onward(dz, dy):
+        open_ways = []
+        if dy == 0 and dz <= 0:
+            open_ways.append(0)
+        if dy == 0 and dz >= 0:
+            open_ways.append(1)
+        if dy <= 0:
+            open_ways.append(2)
+        if dy >= 0:
+            open_ways.append(3)
+        return open_ways
+
+    offsets = sorted(
+        ((dz, dy) for dz in range(1 - z_count, z_count) for dy in range(1 - y_count, y_count)),
+        key=lambda o: (abs(o[0]) + abs(o[1]), abs(o[1])),
+    )
+    true = row >= 0
+    leading = row < 2
+
+    def present(dz, dy):
+        inside = jnp.logical_and(z + dz >= 0, z + dz < z_count)
+        inside = jnp.logical_and(inside, jnp.logical_and(y + dy >= 0, y + dy < y_count))
+        slab = (z + dz) * y_count + y + dy
+        return inside, jnp.where(inside, slab, 0)
+
+    def lead_event(dz, dy):
+        inside, slab = present(dz, dy)
+        mine = jnp.logical_and(inside, leading)
+        half = jnp.where(leading, row, 0)
+        target = leads.at[half, slab]
+        first = dz == 0 and dy == 0
+        if first:
+            keep(mine, grads.at[0, 0], target, local.at[0])
+        else:
+            arrived(mine, target, lead_recv.at[half, slab])
+        source = grads.at[0, 0] if first else target
+        for way in onward(dz, dy):
+            push(jnp.logical_and(mine, steps[way][0]), source, target,
+                 lead_send.at[slab, way], lead_recv.at[half, slab], (row, steps[way][1]))
+        for k, other in enumerate(others):
+            push(mine, source, target, lead_send.at[slab, 4 + k], lead_recv.at[half, slab],
+                 (other, col))
+
+    def rows_event(dz, dy):
+        inside, slab = present(dz, dy)
+        target = rows.at[:, :, slab]
+        first = dz == 0 and dy == 0
+        if first:
+            keep(true, grads, target, local.at[1])
+        else:
+            arrived(inside, target, rows_recv.at[slab])
+        source = grads if first else target
+        for way in onward(dz, dy):
+            push(jnp.logical_and(inside, steps[way][0]), source, target,
+                 rows_send.at[slab, way], rows_recv.at[slab], (row, steps[way][1]))
+        forward = jnp.logical_and(inside, owner)
+        picked = grads.at[:, group] if first else rows.at[:, group, slab]
+        for k, other in enumerate(others):
+            push(forward, picked, cols.at[:, slab], cols_send.at[slab, k], cols_recv.at[slab],
+                 (other, col))
+        keep(forward, picked, cols.at[:, slab], cols_send.at[slab, row_count - 1])
+
+    lead_event(0, 0)
+    for k, other in enumerate(others):
+        push(true, order, orders.at[row], order_send.at[k], order_recv.at[row], (other, col))
+    keep(true, order, orders.at[row], local.at[2])
+    rows_event(0, 0)
+    for offset in offsets[1:]:
+        lead_event(*offset)
+    for offset in offsets[1:]:
+        rows_event(*offset)
+    for half in range(2):
+        for slab in range(col_count):
+            arrived(row != half, leads.at[half, slab], lead_recv.at[half, slab])
+    for other in others:
+        arrived(true, orders.at[other], order_recv.at[other])
+    for slab in range(col_count):
+        arrived(jnp.logical_not(owner), cols.at[:, slab], cols_recv.at[slab])
+    for condition, finish in started:
+        pl.when(condition)(finish)
+
+
+def gather_call(row_count, col_count, grads, order):
+    local_cols, ratio, part, features = grads.shape
+    local_rows, size = order.shape
+    hbm = pl.BlockSpec(memory_space=pl.ANY)
+    dma = pltpu.SemaphoreType.DMA
+    return pl.pallas_call(
+        functools.partial(gather_kernel, row_count, col_count),
+        out_shape=(
+            jax.ShapeDtypeStruct((local_cols, ratio, col_count, part, features), BF16),
+            jax.ShapeDtypeStruct((local_cols, col_count, part, features), BF16),
+            jax.ShapeDtypeStruct((2, col_count, part, features), BF16),
+            jax.ShapeDtypeStruct((row_count, local_rows, size), jnp.int32),
+        ),
+        in_specs=[hbm, hbm],
+        out_specs=(hbm, hbm, hbm, hbm),
+        scratch_shapes=[
+            dma((col_count, 3 + row_count)),
+            dma((col_count, 4)),
+            dma((col_count, row_count)),
+            dma((row_count,)),
+            dma((2, col_count)),
+            dma((col_count,)),
+            dma((col_count,)),
+            dma((row_count,)),
+            dma((3,)),
+        ],
+        compiler_params=pltpu.CompilerParams(collective_id=0, has_side_effects=True),
+        name="gather",
+    )(grads, order)
 
 
 def per_device(gradients, feature_weights, order):
     row_count = lax.axis_size("row")
     col_count = lax.axis_size("col")
-    row_index = lax.axis_index("row")
-    col_index = lax.axis_index("col")
     ratio = col_count // row_count
     local_rows, _, _, part, features = gradients.shape
     size = order.shape[2]
     weights = feature_weights.reshape(1, features)
-    orders = lax.all_gather(order, "row", axis=1, tiled=True)
-    leaders = lax.all_gather(gradients[0, 0], ("row", "col"), axis=0, tiled=False)
-    leaders = leaders.reshape(row_count, size, features)[:2]
-    gathered = lax.all_gather(gradients, "col", axis=2, tiled=True)
-    rows_raw = gathered.reshape(local_rows, size, features)
-    source = col_index % row_count
-
-    def pick(blocks):
-        grouped = blocks.reshape((local_rows // ratio, ratio) + blocks.shape[1:])
-        return lax.dynamic_index_in_dim(grouped, col_index // row_count, axis=1, keepdims=False)
-
-    kept = jnp.where(row_index == source, pick(rows_raw), 0).astype(BF16)
-    cols_raw = lax.psum(kept, "row")
-    cols_order = pick(lax.dynamic_index_in_dim(orders, source, axis=1, keepdims=False))
-    corner = corner_call(leaders, orders[0, :2], weights)
-    place = jnp.stack([row_index, col_index]).astype(jnp.int32)
+    rows, cols, leads, orders = gather_call(
+        row_count, col_count, gradients.reshape(local_rows // ratio, ratio, part, features),
+        order.reshape(local_rows, size),
+    )
+    corner = corner_call(leads.reshape(2, size, features), orders, weights)
     return window_call(
-        row_count, col_count, place, rows_raw, order.reshape(local_rows, size), cols_raw,
-        cols_order, weights, corner,
+        row_count, col_count, rows.reshape(local_rows, size, features), orders,
+        cols.reshape(local_rows // ratio, size, features), weights, corner,
     )
 
 

time: 189 us -> 107 us (0.57)
  waiting for transfers between devices: 103 us -> 0 us
  Pallas kernels: 52.3 us -> 103 us
  between operations: 13.2 us -> 0.05 us
  local copies, waits for them, and re-layouts: 11.8 us -> 3.78 us
  blocking collectives: 6.16 us -> 0 us
  other arithmetic: 2.34 us -> 0 us
    all_gather x2 -> x0, waiting for transfers between devices: 99.7 us -> none  [the longest x1 51.2 us: per_device(): lax.all_gather(gradients[0, 0], ('row', 'col'), axis=0, tiled=False)]
    pallas_call x0 -> x1, Pallas kernels: none -> 51.1 us  [gather_call(): pl.pallas_call(functools.partial(gather_kernel, row_count, col_count), ou...]
    all_gather x1 -> x0, blocking collectives: 6.16 us -> none  [per_device(): orders = lax.all_gather(order, 'row', axis=1, tiled=True)]
    unnamed x23 -> x13, local copies, waits for them, and re-layouts: 8.48 us -> 3.78 us
    slice x3 -> x0, local copies, waits for them, and re-layouts: 3.26 us -> none  [the longest x1 1.88 us: per_device(): leaders = leaders.reshape(row_count, size, features)[:2]]
    psum x1 -> x0, waiting for transfers between devices: 2.58 us -> none  [per_device(): cols_raw = lax.psum(kept, 'row')]
    select_n x1 -> x0, other arithmetic: 2.27 us -> none  [per_device(): kept = jnp.where(row_index == source, pick(rows_raw), 0).astype(BF16)]
  transfers between devices with their start and end apart: 3 -> 0, of which waited for: 3 -> 0; matrix products, arithmetic and copies ran while one was open for 1% -> 0% of each run, Pallas kernels for 15% -> 0%
where the time goes in v2:
time: 107 us
  Pallas kernels  103 us (96%)
  local copies, waits for them, and re-layouts  3.78 us (4%)
    pallas_call x1, Pallas kernels, gather_call(): pl.pallas_call(functools.partial(gather_kernel, row_count, col_count), ou...  51.1 us
    pallas_call x1, Pallas kernels, corner_call(): pl.pallas_call(corner_kernel, out_shape=(jax.ShapeDtypeStruct((whole, fea...  29.1 us
    pallas_call x1, Pallas kernels, window_call(): pl.pallas_call(functools.partial(window_kernel, row_count, col_count), ou...  23 us
    unnamed x13, local copies, waits for them, and re-layouts  3.78 us

profile of v2, /device:TPU:0, one launch (start us, length us, event | category | flops | bytes accessed | tf_op | source)
XLA Modules:
  0.0 107.0 jit_solution(12882214631300500614)
XLA Ops:
  0.0 1.3 %copy.6 = s32[8,1,256]{2,0,1:T(8,128)} copy(s32[8,1,256]{2,1,0:T(1,128)} %param.5) | data formatting | bytes 16384
  1.3 51.1 %gather.1 = (bf16[4,2,8,32,512]{4,3,2,1,0:T(8,128)(2,1)}, bf16[4,8,32,512]{3,2,1,0:T(8,128)(2,1)}, bf16[2,8,32,512]{3,2,1,0:T(8,128)(2,1)}, s32[4,8,256]{2,1,0:T(8,128)}) custom-call(bf16[4,2,32,512]{3,2,1,0:T(8,128)(2,1)} %bitcast.13, s32[8,256]{1,0:T(8,128)} %bitcast.14), custom_call_target="tpu_custom_call" | custom-call | tf_op jit(solution)/shard_map/gather/pallas_call | solution.py:418
  52.4 0.0 copy-start.2
  52.4 0.7 copy-done.2
  53.2 0.0 copy-start.4
  53.2 0.7 copy-done.4
  53.8 0.0 copy-start.5
  53.8 1.0 copy-done.5
  54.9 0.0 copy-start
  54.9 0.0 copy-start.1
  54.9 0.0 copy-start.3
  54.9 29.1 %corner.1 = (bf16[512,512]{1,0:T(8,128)(2,1)S(1)}, f32[8,512]{1,0:T(8,128)S(1)}, f32[512,512]{1,0:T(8,128)S(1)}, bf16[512,512]{1,0:T(8,128)(2,1)S(1)}, bf16[512,512]{1,0:T(8,128)(2,1)S(1)}) custom-call(bf16[2,256,512]{2,1,0:T(8,128)(2,1)S(1)} %bitcast.12, s32[4,8,256]{2,1,0:T(8,128)S(1)} %copy-done.2, f32[1,512]{1,0:T(1,128)S(1)} %bitcast.10), custom_call_target="tpu_custom_call" | custom-call | flops 20000000000 | bytes 4194304 | tf_op jit(solution)/shard_map/corner/pallas_call | solution.py:158
  84.0 0.0 copy-done
  84.0 0.0 copy-done.1
  84.0 0.0 copy-done.3
  84.0 23.0 %window.1 = f32[8,1,4,1,256,256]{5,4,3,2,1,0:T(8,128)} custom-call(bf16[8,256,512]{2,1,0:T(8,128)(2,1)S(1)} %bitcast.8, s32[4,8,256]{2,1,0:T(8,128)S(1)} %copy-done.3, bf16[4,256,512]{2,1,0:T(8,128)(2,1)S(1)} %bitcast.9, f32[1,512]{1,0:T(1,128)S(1)} %bitcast.11, bf16[512,512]{1,0:T(8,128)(2,1)S(1)} %get-tuple-element.18.lead, ...), custom_call_target="tpu_custom_call" | custom-call | tf_op jit(solution)/shard_map/window/pallas_call | solution.py:237
Async XLA Ops:
  52.4 0.8 copy-start.2
  53.2 0.7 copy-start.4
  53.8 1.0 copy-start.5
  54.9 29.1 %copy-start = (bf16[4,2,8,32,512]{4,3,2,1,0:T(8,128)(2,1)S(1)}, bf16[4,2,8,32,512]{4,3,2,1,0:T(8,128)(2,1)}, u32[]{:S(2)}) copy-start(bf16[4,2,8,32,512]{4,3,2,1,0:T(8,128)(2,1)} %get-tuple-element.14) | copy-start | bytes 6291460
  54.9 29.1 %copy-start.1 = (bf16[4,8,32,512]{3,2,1,0:T(8,128)(2,1)S(1)}, bf16[4,8,32,512]{3,2,1,0:T(8,128)(2,1)}, u32[]{:S(2)}) copy-start(bf16[4,8,32,512]{3,2,1,0:T(8,128)(2,1)} %get-tuple-element.16) | copy-start | bytes 3145732
  54.9 29.1 %copy-start.3 = (s32[4,8,256]{2,1,0:T(8,128)S(1)}, s32[4,8,256]{2,1,0:T(8,128)}, u32[]{:S(2)}) copy-start(s32[4,8,256]{2,1,0:T(8,128)} %get-tuple-element.15.order.orders) | copy-start | bytes 98308

commit v3 on v2

--- a/solution.py
+++ b/solution.py
@@ -63,7 +63,7 @@
 
 
 STRIP = 128
-MICRO = 8
+MICRO = 16
 
 
 def factor_strip(work):
@@ -77,17 +77,18 @@
         ]
         for k in range(MICRO):
             pivot = lax.rsqrt(jnp.broadcast_to(lanes[k][k : k + 1, :], (MICRO, 128)))
-            factor = lanes[k] * pivot
-            below = jnp.where(sub > k, factor, 0.0)
+            below = jnp.where(sub > k, lanes[k], 0.0) * (pivot * pivot)
             for j in range(k + 1, MICRO):
-                lanes[j] = lanes[j] - below * jnp.broadcast_to(factor[j : j + 1, :], (MICRO, 128))
-            left_k = left * pivot
-            right_k = right * pivot
+                lanes[j] = lanes[j] - below * jnp.broadcast_to(lanes[k][j : j + 1, :], (MICRO, 128))
             left = jnp.where(
-                sub == k, left_k, left - below * jnp.broadcast_to(left_k[k : k + 1], (MICRO, 128))
+                sub == k,
+                left * pivot,
+                left - below * jnp.broadcast_to(left[k : k + 1], (MICRO, 128)),
             )
             right = jnp.where(
-                sub == k, right_k, right - below * jnp.broadcast_to(right_k[k : k + 1], (MICRO, 128))
+                sub == k,
+                right * pivot,
+                right - below * jnp.broadcast_to(right[k : k + 1], (MICRO, 128)),
             )
         done = jnp.concatenate([left, right], axis=1)
         work[base : base + MICRO, :] = done
@@ -103,12 +104,12 @@
             work[base + MICRO :, :] = work[base + MICRO :, :] - mm(turned, rhs)
 
 
-def corner_kernel(raw, order, weights, cand_out, squares_out, lower_out, inv_high, inv_low,
-                  corner, upper, inverse, work):
-    size = raw.shape[1]
+def corner_body(raw, order, weights, cand_out, squares_out, lower_out, inv_high, inv_low,
+                corner, upper, inverse, work, meanwhile):
+    size = raw.shape[1] * raw.shape[2]
     cands, scaleds, squares = [], [], []
     for block in range(2):
-        cand = ordered(raw[block], order[block, 0:1, :])
+        cand = ordered(raw[block].reshape(size, raw.shape[3]), order[block, 0:1, :])
         scaled, square = scale(cand, weights[...])
         cand_out[block * size : (block + 1) * size, :] = cand
         squares_out[:, block * size : (block + 1) * size] = as_row(square)
@@ -127,6 +128,7 @@
     inverse[...] = jnp.zeros_like(inverse)
 
     def strip(index, _):
+        meanwhile(index)
         own = pl.ds(pl.multiple_of(index * STRIP, STRIP), STRIP)
         left = split(jnp.transpose(upper[:, own]))
         current = corner[own, :] - mm3(mm, left, split(upper[...]))
@@ -152,32 +154,6 @@
     inv_low[...] = low
 
 
-def corner_call(raw, order, weights):
-    size, features = raw.shape[1:]
-    whole = 2 * size
-    return pl.pallas_call(
-        corner_kernel,
-        out_shape=(
-            jax.ShapeDtypeStruct((whole, features), BF16),
-            jax.ShapeDtypeStruct((8, whole), F32),
-            jax.ShapeDtypeStruct((whole, whole), F32),
-            jax.ShapeDtypeStruct((whole, whole), BF16),
-            jax.ShapeDtypeStruct((whole, whole), BF16),
-        ),
-        scratch_shapes=[
-            pltpu.VMEM((whole, whole), F32),
-            pltpu.VMEM((whole, whole), F32),
-            pltpu.VMEM((whole, whole), F32),
-            pltpu.VMEM((STRIP, 2 * STRIP), F32),
-        ],
-        compiler_params=pltpu.CompilerParams(vmem_limit_bytes=24 << 20),
-        cost_estimate=pl.CostEstimate(
-            flops=20_000_000_000, bytes_accessed=4 << 20, transcendentals=0
-        ),
-        name="corner",
-    )(raw, order, weights)
-
-
 def window_kernel(row_count, col_count, rows_raw, orders, cols_raw, weights,
                   lead, lead_squares, lower, inv_high, inv_low, out,
                   col_cand, col_squares, col_high, col_low):
@@ -191,8 +167,15 @@
 
     def panel(scaled, squares, block):
         entries = tile(scaled, squares, lead[...], lead_squares[0:1, :])
-        inverse = (inv_high[...], inv_low[...])
-        solved = mm3(mm_nt, split(entries), inverse)
+        high, low = split(entries)
+        top, bottom = slice(0, size), slice(size, 2 * size)
+        solved = jnp.concatenate(
+            [
+                mm3(mm_nt, (high[:, top], low[:, top]), (inv_high[top, top], inv_low[top, top])),
+                mm3(mm_nt, (high, low), (inv_high[bottom, :], inv_low[bottom, :])),
+            ],
+            axis=1,
+        )
         start = pl.multiple_of(jnp.minimum(block, 1) * size, size)
         return jnp.where(block < 2, lower[pl.ds(start, size), :], solved)
 
@@ -266,7 +249,9 @@
 MESH = pl.DeviceIdType.MESH
 
 
-def gather_kernel(row_count, col_count, grads, order, rows, cols, leads, orders,
+def gather_kernel(row_count, col_count, grads, order, weights, rows, cols, orders,
+                  cand_out, squares_out, lower_out, inv_high, inv_low,
+                  leads, corner, upper, inverse, work,
                   lead_send, rows_send, cols_send, order_send,
                   lead_recv, rows_recv, cols_recv, order_recv, local):
     row, col = lax.axis_index("row"), lax.axis_index("col")
@@ -295,30 +280,20 @@
         expected = expected + jnp.where(inside, 1, 0)
     pl.semaphore_wait(barrier, expected)
 
-    started = []
-
-    def push(condition, source, target, send, receive, device):
-        def copy():
-            return pltpu.make_async_remote_copy(
+    def push(finish, condition, source, target, send, receive, device):
+        @pl.when(condition)
+        def _():
+            copy = pltpu.make_async_remote_copy(
                 src_ref=source, dst_ref=target, send_sem=send, recv_sem=receive,
                 device_id=device, device_id_type=MESH,
             )
-
+            copy.wait_send() if finish else copy.start()
+
+    def keep(finish, condition, source, target, sem):
         @pl.when(condition)
         def _():
-            copy().start()
-
-        started.append((condition, lambda: copy().wait_send()))
-
-    def keep(condition, source, target, sem):
-        def copy():
-            return pltpu.make_async_copy(source, target, sem)
-
-        @pl.when(condition)
-        def _():
-            copy().start()
-
-        started.append((condition, lambda: copy().wait()))
+            copy = pltpu.make_async_copy(source, target, sem)
+            copy.wait() if finish else copy.start()
 
     def arrived(condition, target, receive):
         @pl.when(condition)
@@ -353,79 +328,107 @@
         slab = (z + dz) * y_count + y + dy
         return inside, jnp.where(inside, slab, 0)
 
-    def lead_event(dz, dy):
+    def lead_event(dz, dy, finish=False):
         inside, slab = present(dz, dy)
         mine = jnp.logical_and(inside, leading)
         half = jnp.where(leading, row, 0)
         target = leads.at[half, slab]
         first = dz == 0 and dy == 0
         if first:
-            keep(mine, grads.at[0, 0], target, local.at[0])
-        else:
+            keep(finish, mine, grads.at[0, 0], target, local.at[0])
+        elif not finish:
             arrived(mine, target, lead_recv.at[half, slab])
         source = grads.at[0, 0] if first else target
         for way in onward(dz, dy):
-            push(jnp.logical_and(mine, steps[way][0]), source, target,
+            push(finish, jnp.logical_and(mine, steps[way][0]), source, target,
                  lead_send.at[slab, way], lead_recv.at[half, slab], (row, steps[way][1]))
         for k, other in enumerate(others):
-            push(mine, source, target, lead_send.at[slab, 4 + k], lead_recv.at[half, slab],
+            push(finish, mine, source, target, lead_send.at[slab, 4 + k], lead_recv.at[half, slab],
                  (other, col))
 
-    def rows_event(dz, dy):
+    def rows_event(dz, dy, finish=False):
         inside, slab = present(dz, dy)
         target = rows.at[:, :, slab]
         first = dz == 0 and dy == 0
         if first:
-            keep(true, grads, target, local.at[1])
-        else:
+            keep(finish, true, grads, target, local.at[1])
+        elif not finish:
             arrived(inside, target, rows_recv.at[slab])
         source = grads if first else target
         for way in onward(dz, dy):
-            push(jnp.logical_and(inside, steps[way][0]), source, target,
+            push(finish, jnp.logical_and(inside, steps[way][0]), source, target,
                  rows_send.at[slab, way], rows_recv.at[slab], (row, steps[way][1]))
         forward = jnp.logical_and(inside, owner)
         picked = grads.at[:, group] if first else rows.at[:, group, slab]
         for k, other in enumerate(others):
-            push(forward, picked, cols.at[:, slab], cols_send.at[slab, k], cols_recv.at[slab],
+            push(finish, forward, picked, cols.at[:, slab], cols_send.at[slab, k], cols_recv.at[slab],
                  (other, col))
-        keep(forward, picked, cols.at[:, slab], cols_send.at[slab, row_count - 1])
+        keep(finish, forward, picked, cols.at[:, slab], cols_send.at[slab, row_count - 1])
+
+    def order_event(finish=False):
+        for k, other in enumerate(others):
+            push(finish, true, order, orders.at[row], order_send.at[k], order_recv.at[row],
+                 (other, col))
+        keep(finish, true, order, orders.at[row], local.at[2])
 
     lead_event(0, 0)
-    for k, other in enumerate(others):
-        push(true, order, orders.at[row], order_send.at[k], order_recv.at[row], (other, col))
-    keep(true, order, orders.at[row], local.at[2])
+    order_event()
     rows_event(0, 0)
     for offset in offsets[1:]:
         lead_event(*offset)
-    for offset in offsets[1:]:
-        rows_event(*offset)
     for half in range(2):
         for slab in range(col_count):
             arrived(row != half, leads.at[half, slab], lead_recv.at[half, slab])
     for other in others:
         arrived(true, orders.at[other], order_recv.at[other])
+    for offset in offsets:
+        lead_event(*offset, finish=True)
+    order_event(finish=True)
+    strips = corner.shape[0] // STRIP
+
+    def meanwhile(index):
+        for turn in range(strips):
+            @pl.when(index == turn)
+            def _():
+                for offset in offsets[1:]:
+                    if min(abs(offset[0]) + abs(offset[1]), strips) == turn + 1:
+                        rows_event(*offset)
+
+    corner_body(leads, orders, weights, cand_out, squares_out, lower_out, inv_high, inv_low,
+                corner, upper, inverse, work, meanwhile)
     for slab in range(col_count):
         arrived(jnp.logical_not(owner), cols.at[:, slab], cols_recv.at[slab])
-    for condition, finish in started:
-        pl.when(condition)(finish)
-
-
-def gather_call(row_count, col_count, grads, order):
+    for offset in offsets:
+        rows_event(*offset, finish=True)
+
+
+def gather_call(row_count, col_count, grads, order, weights):
     local_cols, ratio, part, features = grads.shape
     local_rows, size = order.shape
+    whole = 2 * size
     hbm = pl.BlockSpec(memory_space=pl.ANY)
+    vmem = pl.BlockSpec(memory_space=pltpu.VMEM)
     dma = pltpu.SemaphoreType.DMA
     return pl.pallas_call(
         functools.partial(gather_kernel, row_count, col_count),
         out_shape=(
             jax.ShapeDtypeStruct((local_cols, ratio, col_count, part, features), BF16),
             jax.ShapeDtypeStruct((local_cols, col_count, part, features), BF16),
-            jax.ShapeDtypeStruct((2, col_count, part, features), BF16),
             jax.ShapeDtypeStruct((row_count, local_rows, size), jnp.int32),
+            jax.ShapeDtypeStruct((whole, features), BF16),
+            jax.ShapeDtypeStruct((8, whole), F32),
+            jax.ShapeDtypeStruct((whole, whole), F32),
+            jax.ShapeDtypeStruct((whole, whole), BF16),
+            jax.ShapeDtypeStruct((whole, whole), BF16),
         ),
-        in_specs=[hbm, hbm],
-        out_specs=(hbm, hbm, hbm, hbm),
+        in_specs=[hbm, hbm, vmem],
+        out_specs=(hbm, hbm, vmem, vmem, vmem, vmem, vmem, vmem),
         scratch_shapes=[
+            pltpu.VMEM((2, col_count, part, features), BF16),
+            pltpu.VMEM((whole, whole), F32),
+            pltpu.VMEM((whole, whole), F32),
+            pltpu.VMEM((whole, whole), F32),
+            pltpu.VMEM((STRIP, 2 * STRIP), F32),
             dma((col_count, 3 + row_count)),
             dma((col_count, 4)),
             dma((col_count, row_count)),
@@ -436,9 +439,11 @@
             dma((row_count,)),
             dma((3,)),
         ],
-        compiler_params=pltpu.CompilerParams(collective_id=0, has_side_effects=True),
+        compiler_params=pltpu.CompilerParams(
+            collective_id=0, has_side_effects=True, vmem_limit_bytes=32 << 20
+        ),
         name="gather",
-    )(grads, order)
+    )(grads, order, weights)
 
 
 def per_device(gradients, feature_weights, order):
@@ -448,11 +453,10 @@
     local_rows, _, _, part, features = gradients.shape
     size = order.shape[2]
     weights = feature_weights.reshape(1, features)
-    rows, cols, leads, orders = gather_call(
+    rows, cols, orders, *corner = gather_call(
         row_count, col_count, gradients.reshape(local_rows // ratio, ratio, part, features),
-        order.reshape(local_rows, size),
+        order.reshape(local_rows, size), weights,
     )
-    corner = corner_call(leads.reshape(2, size, features), orders, weights)
     return window_call(
         row_count, col_count, rows.reshape(local_rows, size, features), orders,
         cols.reshape(local_rows // ratio, size, features), weights, corner,

time: 107 us -> 73.7 us (0.69)
  the two profiles are of different devices: /device:TPU:0 before, /device:TPU:10 now
where the time goes in v3:
time: 73.7 us; the launch traced here: 73.4 us
  Pallas kernels  70.4 us (96%)
  local copies, waits for them, and re-layouts  3 us (4%)
    pallas_call x1, Pallas kernels, gather_call(): pl.pallas_call(functools.partial(gather_kernel, row_count, col_count), ou...  49.6 us
    pallas_call x1, Pallas kernels, window_call(): pl.pallas_call(functools.partial(window_kernel, row_count, col_count), ou...  20.8 us
    unnamed x7, local copies, waits for them, and re-layouts  3 us

profile of v3, /device:TPU:10, one launch (start us, length us, event | category | flops | bytes accessed | tf_op | source)
XLA Modules:
  0.0 73.4 jit_solution(1130804474170810619)
XLA Ops:
  0.0 0.7 copy.6
  0.7 0.0 copy-start
  0.7 0.9 %copy-done = bf16[8,1,1,32,512]{4,3,2,1,0:T(8,128)(2,1)S(1)} copy-done((bf16[8,1,1,32,512]{4,3,2,1,0:T(8,128)(2,1)S(1)}, bf16[8,1,1,32,512]{4,3,2,1,0:T(8,128)(2,1)}, u32[]{:S(2)}) %copy-start) | copy-done | bytes 262168
  1.6 0.0 copy-start.1
  1.7 0.7 copy-done.1
  2.3 49.6 %gather.1 = (bf16[4,2,8,32,512]{4,3,2,1,0:T(8,128)(2,1)S(1)}, bf16[4,8,32,512]{3,2,1,0:T(8,128)(2,1)S(1)}, s32[4,8,256]{2,1,0:T(8,128)S(1)}, bf16[512,512]{1,0:T...) custom-call(bf16[4,2,32,512]{3,2,1,0:T(8,128)(2,1)S(1)} %bitcast.9, ...), custom_call_target="tpu_custom_call" | custom-call | tf_op jit(solution)/shard_map/gather/pallas_call | solution.py:412
  51.9 0.0 copy-start.2
  51.9 0.7 copy-done.2
  52.6 20.8 %window.1 = f32[8,1,4,1,256,256]{5,4,3,2,1,0:T(8,128)} custom-call(bf16[8,256,512]{2,1,0:T(8,128)(2,1)S(1)} %bitcast.7, s32[4,8,256]{2,1,0:T(8,128)S(1)} %get-tuple-element.14.orders, bf16[4,256,512]{2,1,0:T(8,128)(2,1)S(1)} %bitcast.8, f32[1,512]{1,0:T(1,128)S(1)} %bitcast.12, bf16[512,512]{1,0:T(8,128)(2,1)S(1)} %get-tuple-element.16.lead, ...), custom_call_target="tpu_custom_call" | custom-call | tf_op jit(solution)/shard_map/window/pallas_call | solution.py:220
Async XLA Ops:
  0.7 0.9 %copy-start = (bf16[8,1,1,32,512]{4,3,2,1,0:T(8,128)(2,1)S(1)}, bf16[8,1,1,32,512]{4,3,2,1,0:T(8,128)(2,1)}, u32[]{:S(2)}) copy-start(bf16[8,1,1,32,512]{4,3,2,1,0:T(8,128)(2,1)} %param.3) | copy-start | bytes 786436
  1.6 0.7 copy-start.1
  51.9 0.7 copy-start.2

commit v4 on v3

--- a/solution.py
+++ b/solution.py
@@ -156,7 +156,7 @@
 
 def window_kernel(row_count, col_count, rows_raw, orders, cols_raw, weights,
                   lead, lead_squares, lower, inv_high, inv_low, out,
-                  col_cand, col_squares, col_high, col_low):
+                  col_cand, col_squares, col_stack, inv_first, inv_second):
     step = pl.program_id(0)
     row_index, col_index = lax.axis_index("row"), lax.axis_index("col")
     ratio = col_count // row_count
@@ -168,19 +168,22 @@
     def panel(scaled, squares, block):
         entries = tile(scaled, squares, lead[...], lead_squares[0:1, :])
         high, low = split(entries)
-        top, bottom = slice(0, size), slice(size, 2 * size)
-        solved = jnp.concatenate(
-            [
-                mm3(mm_nt, (high[:, top], low[:, top]), (inv_high[top, top], inv_low[top, top])),
-                mm3(mm_nt, (high, low), (inv_high[bottom, :], inv_low[bottom, :])),
-            ],
-            axis=1,
-        )
+        stacked = jnp.concatenate([high[:, :size], high[:, :size], low[:, :size]], axis=1)
+        first = mm_nt(stacked, inv_first[...])
+        second = mm_nt(jnp.concatenate([high, high, low], axis=1), inv_second[...])
+        solved = jnp.concatenate([first, second], axis=1)
         start = pl.multiple_of(jnp.minimum(block, 1) * size, size)
         return jnp.where(block < 2, lower[pl.ds(start, size), :], solved)
 
     @pl.when(step == 0)
     def _():
+        top, bottom = slice(0, size), slice(size, 2 * size)
+        inv_first[...] = jnp.concatenate(
+            [inv_high[top, top], inv_low[top, top], inv_high[top, top]], axis=1
+        )
+        inv_second[...] = jnp.concatenate(
+            [inv_high[bottom, :], inv_low[bottom, :], inv_high[bottom, :]], axis=1
+        )
         for b in range(local_cols):
             own = slice(b * size, (b + 1) * size)
             cand = ordered(cols_raw[b], orders[source, pl.ds(b * ratio + group, 1), :])
@@ -188,18 +191,18 @@
             high, low = split(panel(scaled, squares, b * col_count + col_index))
             col_cand[own, :] = cand
             col_squares[:, own] = as_row(squares)
-            col_high[own, :] = high
-            col_low[own, :] = low
+            col_stack[own, :] = jnp.concatenate([high, low, high], axis=1)
 
     cand = ordered(rows_raw[0], orders[row_index, pl.ds(step, 1), :])
     scaled, squares = scale(cand, weights[...])
     factors = panel(scaled, squares, label)
-    halves = split(factors)
+    high, low = split(factors)
+    halves = jnp.concatenate([high, high, low], axis=1)
     for b in range(local_cols):
         own = slice(b * size, (b + 1) * size)
         column = b * col_count + col_index
         entries = tile(scaled, squares, col_cand[own, :], col_squares[0:1, own])
-        entries = entries - mm3(mm_nt, halves, (col_high[own, :], col_low[own, :]))
+        entries = entries - mm_nt(halves, col_stack[own, :])
         ridge = jnp.where(label == column, RIDGE, 0.0)
         entries = entries + jnp.where(eye(size), ridge, 0.0)
         entries = jnp.where(label < 2, 0.0, entries)
@@ -238,8 +241,9 @@
         scratch_shapes=[
             pltpu.VMEM((local_cols * size, features), BF16),
             pltpu.VMEM((8, local_cols * size), F32),
-            pltpu.VMEM((local_cols * size, whole), BF16),
-            pltpu.VMEM((local_cols * size, whole), BF16),
+            pltpu.VMEM((local_cols * size, 3 * whole), BF16),
+            pltpu.VMEM((size, 3 * size), BF16),
+            pltpu.VMEM((size, 3 * whole), BF16),
         ],
         compiler_params=pltpu.CompilerParams(vmem_limit_bytes=40 << 20),
         name="window",
@@ -373,9 +377,9 @@
 
     lead_event(0, 0)
     order_event()
-    rows_event(0, 0)
     for offset in offsets[1:]:
         lead_event(*offset)
+    rows_event(0, 0)
     for half in range(2):
         for slab in range(col_count):
             arrived(row != half, leads.at[half, slab], lead_recv.at[half, slab])
@@ -421,7 +425,7 @@
             jax.ShapeDtypeStruct((whole, whole), BF16),
             jax.ShapeDtypeStruct((whole, whole), BF16),
         ),
-        in_specs=[hbm, hbm, vmem],
+        in_specs=[pl.BlockSpec(memory_space=pltpu.HBM), hbm, vmem],
         out_specs=(hbm, hbm, vmem, vmem, vmem, vmem, vmem, vmem),
         scratch_shapes=[
             pltpu.VMEM((2, col_count, part, features), BF16),

time: 73.7 us -> 72.1 us (0.978)
  the two profiles are of different devices: /device:TPU:10 before, /device:TPU:0 now
where the time goes in v4:
time: 72.1 us; the launch traced here: 71.8 us
  Pallas kernels  68.8 us (95%)
  local copies, waits for them, and re-layouts  3 us (4%)
    pallas_call x1, Pallas kernels, gather_call(): pl.pallas_call(functools.partial(gather_kernel, row_count, col_count), ou...  48.3 us
    pallas_call x1, Pallas kernels, window_call(): pl.pallas_call(functools.partial(window_kernel, row_count, col_count), ou...  20.5 us
    unnamed x7, local copies, waits for them, and re-layouts  3 us

profile of v4, /device:TPU:0, one launch (start us, length us, event | category | flops | bytes accessed | tf_op | source)
XLA Modules:
  0.0 71.8 jit_solution(13138762502150021798)
XLA Ops:
  0.0 0.7 copy.6
  0.7 0.0 copy-start
  0.7 0.9 %copy-done = bf16[8,1,1,32,512]{4,3,2,1,0:T(8,128)(2,1)S(1)} copy-done((bf16[8,1,1,32,512]{4,3,2,1,0:T(8,128)(2,1)S(1)}, bf16[8,1,1,32,512]{4,3,2,1,0:T(8,128)(2,1)}, u32[]{:S(2)}) %copy-start) | copy-done | bytes 262168
  1.6 0.0 copy-start.1
  1.7 0.7 copy-done.1
  2.3 48.3 %gather.1 = (bf16[4,2,8,32,512]{4,3,2,1,0:T(8,128)(2,1)S(1)}, bf16[4,8,32,512]{3,2,1,0:T(8,128)(2,1)S(1)}, s32[4,8,256]{2,1,0:T(8,128)S(1)}, bf16[512,512]{1,0:T...) custom-call(bf16[4,2,32,512]{3,2,1,0:T(8,128)(2,1)S(1)} %bitcast.9, ...), custom_call_target="tpu_custom_call" | custom-call | tf_op jit(solution)/shard_map/gather/pallas_call | solution.py:416
  50.7 0.0 copy-start.2
  50.7 0.7 copy-done.2
  51.4 20.5 %window.1 = f32[8,1,4,1,256,256]{5,4,3,2,1,0:T(8,128)} custom-call(bf16[8,256,512]{2,1,0:T(8,128)(2,1)S(1)} %bitcast.7, s32[4,8,256]{2,1,0:T(8,128)S(1)} %get-tuple-element.14.orders, bf16[4,256,512]{2,1,0:T(8,128)(2,1)S(1)} %bitcast.8, f32[1,512]{1,0:T(1,128)S(1)} %bitcast.12, bf16[512,512]{1,0:T(8,128)(2,1)S(1)} %get-tuple-element.16.lead, ...), custom_call_target="tpu_custom_call" | custom-call | tf_op jit(solution)/shard_map/window/pallas_call | solution.py:223
Async XLA Ops:
  0.7 0.9 %copy-start = (bf16[8,1,1,32,512]{4,3,2,1,0:T(8,128)(2,1)S(1)}, bf16[8,1,1,32,512]{4,3,2,1,0:T(8,128)(2,1)}, u32[]{:S(2)}) copy-start(bf16[8,1,1,32,512]{4,3,2,1,0:T(8,128)(2,1)} %param.3) | copy-start | bytes 786436
  1.6 0.7 copy-start.1
  50.7 0.7 copy-start.2

commit v5 on v4

--- a/solution.py
+++ b/solution.py
@@ -63,6 +63,7 @@
 
 
 STRIP = 128
+PAIR = 2
 MICRO = 16
 
 
@@ -163,15 +164,16 @@
     source, group = lax.rem(col_index, row_count), lax.div(col_index, row_count)
     size = rows_raw.shape[1]
     local_cols = cols_raw.shape[0]
-    label = step * row_count + row_index
-
-    def panel(scaled, squares, block):
+
+    def solve(scaled, squares):
         entries = tile(scaled, squares, lead[...], lead_squares[0:1, :])
         high, low = split(entries)
         stacked = jnp.concatenate([high[:, :size], high[:, :size], low[:, :size]], axis=1)
         first = mm_nt(stacked, inv_first[...])
         second = mm_nt(jnp.concatenate([high, high, low], axis=1), inv_second[...])
-        solved = jnp.concatenate([first, second], axis=1)
+        return jnp.concatenate([first, second], axis=1)
+
+    def placed(solved, block):
         start = pl.multiple_of(jnp.minimum(block, 1) * size, size)
         return jnp.where(block < 2, lower[pl.ds(start, size), :], solved)
 
@@ -188,28 +190,36 @@
             own = slice(b * size, (b + 1) * size)
             cand = ordered(cols_raw[b], orders[source, pl.ds(b * ratio + group, 1), :])
             scaled, squares = scale(cand, weights[...])
-            high, low = split(panel(scaled, squares, b * col_count + col_index))
+            high, low = split(placed(solve(scaled, squares), b * col_count + col_index))
             col_cand[own, :] = cand
             col_squares[:, own] = as_row(squares)
             col_stack[own, :] = jnp.concatenate([high, low, high], axis=1)
 
-    cand = ordered(rows_raw[0], orders[row_index, pl.ds(step, 1), :])
+    pair = [PAIR * step + half for half in range(PAIR)]
+    cand = jnp.concatenate(
+        [ordered(rows_raw[half], orders[row_index, pl.ds(at, 1), :]) for half, at in enumerate(pair)]
+    )
     scaled, squares = scale(cand, weights[...])
-    factors = panel(scaled, squares, label)
+    solved = solve(scaled, squares)
+    labels = [at * row_count + row_index for at in pair]
+    spans = [slice(half * size, (half + 1) * size) for half in range(PAIR)]
+    factors = jnp.concatenate([placed(solved[span], label) for span, label in zip(spans, labels)])
     high, low = split(factors)
     halves = jnp.concatenate([high, high, low], axis=1)
     for b in range(local_cols):
         own = slice(b * size, (b + 1) * size)
         column = b * col_count + col_index
-        entries = tile(scaled, squares, col_cand[own, :], col_squares[0:1, own])
-        entries = entries - mm_nt(halves, col_stack[own, :])
-        ridge = jnp.where(label == column, RIDGE, 0.0)
-        entries = entries + jnp.where(eye(size), ridge, 0.0)
-        entries = jnp.where(label < 2, 0.0, entries)
-        if b == 0:
-            lead_part = jnp.where(column == 0, factors[:, :size], factors[:, size:])
-            entries = jnp.where(column < 2, lead_part, entries)
-        out[0, 0, b, 0] = entries
+        both = tile(scaled, squares, col_cand[own, :], col_squares[0:1, own])
+        both = both - mm_nt(halves, col_stack[own, :])
+        for half, label in enumerate(labels):
+            ridge = jnp.where(label == column, RIDGE, 0.0)
+            entries = both[spans[half]] + jnp.where(eye(size), ridge, 0.0)
+            entries = jnp.where(label < 2, 0.0, entries)
+            if b == 0:
+                part = factors[spans[half]]
+                lead_part = jnp.where(column == 0, part[:, :size], part[:, size:])
+                entries = jnp.where(column < 2, lead_part, entries)
+            out[half, 0, b, 0] = entries
 
 
 def window_call(row_count, col_count, rows_raw, orders, cols_raw, weights, corner):
@@ -223,9 +233,9 @@
     return pl.pallas_call(
         functools.partial(window_kernel, row_count, col_count),
         out_shape=jax.ShapeDtypeStruct((local_rows, 1, local_cols, 1, size, size), F32),
-        grid=(local_rows,),
+        grid=(local_rows // PAIR,),
         in_specs=[
-            pl.BlockSpec((1, size, features), lambda i: (i, 0, 0)),
+            pl.BlockSpec((PAIR, size, features), lambda i: (i, 0, 0)),
             fixed((row_count, local_rows, size)),
             fixed((local_cols, size, features)),
             fixed((1, features)),
@@ -236,7 +246,7 @@
             fixed((whole, whole)),
         ],
         out_specs=pl.BlockSpec(
-            (1, 1, local_cols, 1, size, size), lambda i: (i, 0, 0, 0, 0, 0)
+            (PAIR, 1, local_cols, 1, size, size), lambda i: (i, 0, 0, 0, 0, 0)
         ),
         scratch_shapes=[
             pltpu.VMEM((local_cols * size, features), BF16),

time: 72.1 us -> 70.9 us (0.983)
  Pallas kernels: 68.8 us -> 67.6 us
    pallas_call x1, Pallas kernels: 20.5 us -> 19.3 us  [window_call(): pl.pallas_call(functools.partial(window_kernel, row_count, col_count), ou...]
where the time goes in v5:
time: 70.9 us; the launch traced here: 70.6 us
  Pallas kernels  67.6 us (95%)
  local copies, waits for them, and re-layouts  3 us (4%)
    pallas_call x1, Pallas kernels, gather_call(): pl.pallas_call(functools.partial(gather_kernel, row_count, col_count), ou...  48.3 us
    pallas_call x1, Pallas kernels, window_call(): pl.pallas_call(functools.partial(window_kernel, row_count, col_count), ou...  19.3 us
    unnamed x7, local copies, waits for them, and re-layouts  3 us

profile of v5, /device:TPU:0, one launch (start us, length us, event | category | flops | bytes accessed | tf_op | source)
XLA Modules:
  0.0 70.6 jit_solution(16549689979979405733)
XLA Ops:
  0.0 0.7 copy.6
  0.7 0.0 copy-start
  0.7 0.9 %copy-done = bf16[8,1,1,32,512]{4,3,2,1,0:T(8,128)(2,1)S(1)} copy-done((bf16[8,1,1,32,512]{4,3,2,1,0:T(8,128)(2,1)S(1)}, bf16[8,1,1,32,512]{4,3,2,1,0:T(8,128)(2,1)}, u32[]{:S(2)}) %copy-start) | copy-done | bytes 262168
  1.6 0.0 copy-start.1
  1.7 0.7 copy-done.1
  2.3 48.3 %gather.1 = (bf16[4,2,8,32,512]{4,3,2,1,0:T(8,128)(2,1)S(1)}, bf16[4,8,32,512]{3,2,1,0:T(8,128)(2,1)S(1)}, s32[4,8,256]{2,1,0:T(8,128)S(1)}, bf16[512,512]{1,0:T...) custom-call(bf16[4,2,32,512]{3,2,1,0:T(8,128)(2,1)S(1)} %bitcast.9, ...), custom_call_target="tpu_custom_call" | custom-call | tf_op jit(solution)/shard_map/gather/pallas_call | solution.py:426
  50.7 0.0 copy-start.2
  50.7 0.7 copy-done.2
  51.4 19.3 %window.1 = f32[8,1,4,1,256,256]{5,4,3,2,1,0:T(8,128)} custom-call(bf16[8,256,512]{2,1,0:T(8,128)(2,1)S(1)} %bitcast.7, s32[4,8,256]{2,1,0:T(8,128)S(1)} %get-tuple-element.14.orders, bf16[4,256,512]{2,1,0:T(8,128)(2,1)S(1)} %bitcast.8, f32[1,512]{1,0:T(1,128)S(1)} %bitcast.12, bf16[512,512]{1,0:T(8,128)(2,1)S(1)} %get-tuple-element.16.lead, ...), custom_call_target="tpu_custom_call" | custom-call | tf_op jit(solution)/shard_map/window/pallas_call | solution.py:233
Async XLA Ops:
  0.7 0.9 %copy-start = (bf16[8,1,1,32,512]{4,3,2,1,0:T(8,128)(2,1)S(1)}, bf16[8,1,1,32,512]{4,3,2,1,0:T(8,128)(2,1)}, u32[]{:S(2)}) copy-start(bf16[8,1,1,32,512]{4,3,2,1,0:T(8,128)(2,1)} %param.3) | copy-start | bytes 786436
  1.6 0.7 copy-start.1
  50.7 0.7 copy-start.2
